TPU v7x, 32 devices: a whole 2x2x4 slice. The times are simulated.
32 devices in a mesh: dp: 2 (over core), fsdp: 16 (over z, y, x).
Axes of the slice: x: 2, y: 2, z: 4, core: 2. Of those that a mesh axis runs over, the one named last changes fastest.
Arguments:
- tokens: bfloat16 [38080, 768], P(('dp', 'fsdp')), may hold values from -6 to 6
- cotangent: bfloat16 [38080, 768], P(('dp', 'fsdp')), may hold values from -6 to 6
- segments: int32 [38080], P(('dp', 'fsdp')), may hold values from 0 to 1, as said below
- padding: int32 [38080], P(('dp', 'fsdp')), may hold values from 0 to 1, as said below
- qkv_weight: float32 [768, 2304], P(('dp', 'fsdp')), may hold values from -0.21875 to 0.21875
- qkv_moment: float32 [768, 2304], P(('dp', 'fsdp')), may hold values from -702.5075 to 702.5075
- qkv_average: float32 [768, 2304], P(('dp', 'fsdp')), may hold values from -0.21875 to 0.21875
- merge_weight: float32 [768, 768], P(('dp', 'fsdp')), may hold values from -2.5 to 2.5
- merge_moment: float32 [768, 768], P(('dp', 'fsdp')), may hold values from -81.959206 to 81.959206
- merge_average: float32 [768, 768], P(('dp', 'fsdp')), may hold values from -2.5 to 2.5
- expand_weight: float32 [768, 3072], P(('dp', 'fsdp')), may hold values from -0.21875 to 0.21875
- expand_moment: float32 [768, 3072], P(('dp', 'fsdp')), may hold values from -351.25375 to 351.25375
- expand_average: float32 [768, 3072], P(('dp', 'fsdp')), may hold values from -0.21875 to 0.21875
- shrink_weight: float32 [3072, 768], P(('dp', 'fsdp')), may hold values from -0.109375 to 0.109375
- shrink_moment: float32 [3072, 768], P(('dp', 'fsdp')), may hold values from -702.5075 to 702.5075
- shrink_average: float32 [3072, 768], P(('dp', 'fsdp')), may hold values from -0.109375 to 0.109375
- small_params: float32 [9216], P(('dp', 'fsdp')), may hold values from -0.4 to 1.4
- small_moment: float32 [9216], P(('dp', 'fsdp')), may hold values from -585.4229 to 585.4229
- small_average: float32 [9216], P(('dp', 'fsdp')), may hold values from -0.4 to 1.4
Outputs:
- activations: bfloat16 [38080, 768], P(('dp', 'fsdp'))
- input_grad: float32 [38080, 768], P(('dp', 'fsdp'))
- qkv_grad: float32 [768, 2304], P(('dp', 'fsdp'))
- qkv_newmoment: float32 [768, 2304], P(('dp', 'fsdp'))
- qkv_updated: float32 [768, 2304], P(('dp', 'fsdp'))
- qkv_newaverage: float32 [768, 2304], P(('dp', 'fsdp'))
- qkv_lowcopy: bfloat16 [768, 2304], P(('dp', 'fsdp'))
- merge_grad: float32 [768, 768], P(('dp', 'fsdp'))
- merge_newmoment: float32 [768, 768], P(('dp', 'fsdp'))
- merge_updated: float32 [768, 768], P(('dp', 'fsdp'))
- merge_newaverage: float32 [768, 768], P(('dp', 'fsdp'))
- merge_lowcopy: bfloat16 [768, 768], P(('dp', 'fsdp'))
- expand_grad: float32 [768, 3072], P(('dp', 'fsdp'))
- expand_newmoment: float32 [768, 3072], P(('dp', 'fsdp'))
- expand_updated: float32 [768, 3072], P(('dp', 'fsdp'))
- expand_newaverage: float32 [768, 3072], P(('dp', 'fsdp'))
- expand_lowcopy: bfloat16 [768, 3072], P(('dp', 'fsdp'))
- shrink_grad: float32 [3072, 768], P(('dp', 'fsdp'))
- shrink_newmoment: float32 [3072, 768], P(('dp', 'fsdp'))
- shrink_updated: float32 [3072, 768], P(('dp', 'fsdp'))
- shrink_newaverage: float32 [3072, 768], P(('dp', 'fsdp'))
- shrink_lowcopy: bfloat16 [3072, 768], P(('dp', 'fsdp'))
- small_grad: float32 [9216], P(('dp', 'fsdp'))
- small_newmoment: float32 [9216], P(('dp', 'fsdp'))
- small_updated: float32 [9216], P(('dp', 'fsdp'))
- small_newaverage: float32 [9216], P(('dp', 'fsdp'))
- small_lowcopy: bfloat16 [9216], P(('dp', 'fsdp'))
Inputs may be any that keep to these rules, and one draw needn't show every extreme that they name: `segments`: on a quarter of the devices, drawn from the seed, all 1190 slots have segment 0 (one full clip). On every other device slots 0 to 471 have segment 0 and the slots from 472 on have segment 1. `padding`: on the full-clip devices of segments every slot is 1; on the others the first 944 slots are 1 and the rest 0.
All inputs are finite; a program needn't handle non-finite values.
Results may differ from a plain program's by a relative error of at most 0.012.
Values may be sent and summed in bfloat16 or wider, within the bound.
A program may use at most 192 MiB of HBM per device.

v0:
```python
from functools import partial

import jax
import jax.numpy as jnp
from jax import lax
from jax.sharding import PartitionSpec as P

D = 768
HEAD_DIM = 64
FF = 3072


epsilon = 1e-06
root_half = 0.7071067811865476
inverse_root_tau = 0.3989422804014327


def normalize_keep(values, gain_vector, shift_vector):
    centred = values - jnp.mean(values, axis=-1, keepdims=True)
    inverse = lax.rsqrt(jnp.mean(centred * centred, axis=-1, keepdims=True) + epsilon)
    scaled = centred * inverse
    return (scaled * gain_vector + shift_vector, scaled, inverse)


def normalize_back(upstream, scaled, inverse, gain_vector):
    weighted = upstream * gain_vector
    centred = weighted - jnp.mean(weighted, axis=-1, keepdims=True)
    result = inverse * (centred - scaled * jnp.mean(weighted * scaled, axis=-1, keepdims=True))
    return (result, jnp.sum(upstream * scaled, axis=0), jnp.sum(upstream, axis=0))


def pairs_of(values):
    return values.reshape(values.shape[0], -1, 2, HEAD_DIM).transpose(1, 0, 2, 3)


def joined_back(values):
    return values.transpose(1, 0, 2, 3).reshape(values.shape[1], -1)


def pair_forward(allowed, pieces):
    query_pair, key_pair, value_pair = pieces
    scores = jnp.einsum(
        "qhd,khd->hqk", query_pair, key_pair, preferred_element_type=jnp.float32
    ) * HEAD_DIM ** (-0.5)
    masked = jnp.where(allowed[None], scores, -1e30)
    highest_score = jnp.max(masked, axis=-1, keepdims=True)
    shifted_exp = jnp.exp(masked - highest_score)
    totals = jnp.sum(shifted_exp, axis=-1, keepdims=True)
    weights = (shifted_exp / totals).astype(jnp.bfloat16)
    attended = jnp.einsum("hqk,khd->qhd", weights, value_pair, preferred_element_type=jnp.float32)
    return (attended.astype(jnp.bfloat16), highest_score[..., 0] + jnp.log(totals[..., 0]))


def pair_backward(allowed, pieces):
    query_pair, key_pair, value_pair, upstream_pair, logsum = pieces
    scores = jnp.einsum(
        "qhd,khd->hqk", query_pair, key_pair, preferred_element_type=jnp.float32
    ) * HEAD_DIM ** (-0.5)
    probs = jnp.where(allowed[None], jnp.exp(scores - logsum[..., None]), 0.0)
    weights = probs.astype(jnp.bfloat16)
    prob_grad = jnp.einsum(
        "qhd,khd->hqk", upstream_pair, value_pair, preferred_element_type=jnp.float32
    )
    value_grad = jnp.einsum(
        "hqk,qhd->khd", weights, upstream_pair, preferred_element_type=jnp.float32
    )
    row_terms = jnp.sum(probs * prob_grad, axis=-1, keepdims=True)
    score_grad = (probs * (prob_grad - row_terms)).astype(jnp.bfloat16)
    query_grad = jnp.einsum(
        "hqk,khd->qhd", score_grad, key_pair, preferred_element_type=jnp.float32
    ) * HEAD_DIM ** (-0.5)
    key_grad = jnp.einsum(
        "hqk,qhd->khd", score_grad, query_pair, preferred_element_type=jnp.float32
    ) * HEAD_DIM ** (-0.5)
    return (query_grad, key_grad, value_grad)


def gather_all(lowered):
    qkv_piece, merge_piece, expand_piece, shrink_piece, small_piece = lowered
    gathered = (
        lax.all_gather(qkv_piece, ("dp", "fsdp"), axis=0, tiled=True),
        lax.all_gather(merge_piece, ("dp", "fsdp"), axis=0, tiled=True),
        lax.all_gather(expand_piece, ("dp", "fsdp"), axis=0, tiled=True),
        lax.all_gather(shrink_piece, ("dp", "fsdp"), axis=0, tiled=True),
        lax.all_gather(small_piece, ("dp", "fsdp"), axis=0, tiled=True),
    )
    return gathered


def split_vectors(small_full):
    columns = small_full.astype(jnp.float32).reshape(D, 8 + FF // D)
    pieces = [columns[:, number] for number in range(8)]
    return (pieces, columns[:, 8:].T.reshape(FF))


def per_device(
    tokens,
    cotangent,
    segments,
    padding,
    qkv_weight,
    qkv_moment,
    qkv_average,
    merge_weight,
    merge_moment,
    merge_average,
    expand_weight,
    expand_moment,
    expand_average,
    shrink_weight,
    shrink_moment,
    shrink_average,
    small_params,
    small_moment,
    small_average,
):
    masters = (qkv_weight, merge_weight, expand_weight, shrink_weight, small_params)
    lowered = tuple((master.astype(jnp.bfloat16) for master in masters))
    bundle = gather_all(lowered)
    qkv_full, merge_full, expand_full, shrink_full, small_full = bundle
    pieces, bias_expand = split_vectors(small_full)
    gain_one, shift_one, bias_query, bias_value, bias_merge, gain_two, shift_two, bias_shrink = (
        pieces
    )
    inputs = tokens.astype(jnp.float32)
    allowed = (segments[:, None] == segments[None, :]) & (padding[:, None] == padding[None, :])
    norm_one, scaled_one, inverse_one = normalize_keep(inputs, gain_one, shift_one)
    norm_one_low = norm_one.astype(jnp.bfloat16)
    joined = jnp.dot(norm_one_low, qkv_full, preferred_element_type=jnp.float32)
    joined = joined + jnp.concatenate([bias_query, jnp.zeros((D,), jnp.float32), bias_value])
    joined_low = joined.astype(jnp.bfloat16)
    query_pairs = pairs_of(joined_low[:, :D])
    key_pairs = pairs_of(joined_low[:, D : 2 * D])
    value_pairs = pairs_of(joined_low[:, 2 * D :])
    attended_pairs, logsums = lax.map(
        partial(pair_forward, allowed), (query_pairs, key_pairs, value_pairs)
    )
    attended_low = joined_back(attended_pairs)
    middle = (
        inputs + jnp.dot(attended_low, merge_full, preferred_element_type=jnp.float32) + bias_merge
    )
    norm_two, scaled_two, inverse_two = normalize_keep(middle, gain_two, shift_two)
    norm_two_low = norm_two.astype(jnp.bfloat16)
    before = jnp.dot(norm_two_low, expand_full, preferred_element_type=jnp.float32) + bias_expand
    after_low = jax.nn.gelu(before, approximate=False).astype(jnp.bfloat16)
    output = (
        middle + jnp.dot(after_low, shrink_full, preferred_element_type=jnp.float32) + bias_shrink
    )
    activations = output.astype(jnp.bfloat16)
    back_full = gather_all(lowered)
    qkv_back, merge_back, expand_back, shrink_back, small_back = back_full
    back_pieces, unused_bias = split_vectors(small_back)
    back_gain_one = back_pieces[0]
    back_gain_two = back_pieces[5]
    outgoing = cotangent.astype(jnp.float32) * padding[:, None].astype(jnp.float32)
    outgoing_low = outgoing.astype(jnp.bfloat16)
    shrink_part = jnp.einsum(
        "sf,sd->fd", after_low, outgoing_low, preferred_element_type=jnp.float32
    )
    shrink_bias_part = jnp.sum(outgoing, axis=0)
    act_grad = jnp.einsum(
        "sd,fd->sf", outgoing_low, shrink_back, preferred_element_type=jnp.float32
    )
    cumulative = 0.5 * (1.0 + lax.erf(before * root_half))
    density = jnp.exp(-0.5 * before * before) * inverse_root_tau
    before_grad = (act_grad * (cumulative + before * density)).astype(jnp.bfloat16)
    expand_part = jnp.einsum(
        "sd,sf->df", norm_two_low, before_grad, preferred_element_type=jnp.float32
    )
    expand_bias_part = jnp.sum(before_grad.astype(jnp.float32), axis=0)
    up_two = jnp.einsum("sf,df->sd", before_grad, expand_back, preferred_element_type=jnp.float32)
    second_back, gain_two_part, shift_two_part = normalize_back(
        up_two, scaled_two, inverse_two, back_gain_two
    )
    middle_grad = outgoing + second_back
    middle_low = middle_grad.astype(jnp.bfloat16)
    merge_part = jnp.einsum(
        "sd,se->de", attended_low, middle_low, preferred_element_type=jnp.float32
    )
    merge_bias_part = jnp.sum(middle_low.astype(jnp.float32), axis=0)
    attended_grad = jnp.einsum(
        "se,de->sd", middle_low, merge_back, preferred_element_type=jnp.float32
    ).astype(jnp.bfloat16)
    query_grads, key_grads, value_grads = lax.map(
        partial(pair_backward, allowed),
        (query_pairs, key_pairs, value_pairs, pairs_of(attended_grad), logsums),
    )
    qkv_grad_low = jnp.concatenate(
        [joined_back(query_grads), joined_back(key_grads), joined_back(value_grads)], axis=1
    ).astype(jnp.bfloat16)
    qkv_part = jnp.einsum(
        "sd,sc->dc", norm_one_low, qkv_grad_low, preferred_element_type=jnp.float32
    )
    column_sums = jnp.sum(qkv_grad_low.astype(jnp.float32), axis=0)
    up_one = jnp.einsum("sc,dc->sd", qkv_grad_low, qkv_back, preferred_element_type=jnp.float32)
    first_back, gain_one_part, shift_one_part = normalize_back(
        up_one, scaled_one, inverse_one, back_gain_one
    )
    input_grad = middle_grad + first_back
    vector_rows = jnp.stack(
        [
            gain_one_part,
            shift_one_part,
            column_sums[:D],
            column_sums[2 * D :],
            merge_bias_part,
            gain_two_part,
            shift_two_part,
            shrink_bias_part,
        ]
    )
    all_rows = jnp.concatenate([vector_rows, expand_bias_part.reshape(FF // D, D)], axis=0)
    small_part = all_rows.T.reshape(-1)
    summed = (
        lax.psum_scatter(qkv_part, ("dp", "fsdp"), scatter_dimension=0, tiled=True),
        lax.psum_scatter(merge_part, ("dp", "fsdp"), scatter_dimension=0, tiled=True),
        lax.psum_scatter(expand_part, ("dp", "fsdp"), scatter_dimension=0, tiled=True),
        lax.psum_scatter(shrink_part, ("dp", "fsdp"), scatter_dimension=0, tiled=True),
        lax.psum_scatter(small_part, ("dp", "fsdp"), scatter_dimension=0, tiled=True),
    )
    rate_scale = (tokens.shape[0] * lax.axis_size("dp") * lax.axis_size("fsdp")) ** (-0.5)
    rates = (
        0.04 * rate_scale,
        4.0 * rate_scale,
        0.08 * rate_scale,
        0.02 * rate_scale,
        0.07 * rate_scale,
    )
    moments = (qkv_moment, merge_moment, expand_moment, shrink_moment, small_moment)
    averages = (qkv_average, merge_average, expand_average, shrink_average, small_average)
    results = [activations, input_grad]
    for master, gradient, moment, average, step_rate in zip(
        masters, summed, moments, averages, rates
    ):
        fresh_moment = 0.5 * moment + gradient
        updated = master - step_rate * (gradient + 0.5 * fresh_moment)
        results.extend(
            [
                gradient,
                fresh_moment,
                updated,
                0.5 * average + 0.5 * updated,
                updated.astype(jnp.bfloat16),
            ]
        )
    return tuple(results)


def solution(mesh):
    placed = (
        P(("dp", "fsdp"), None),
        P(("dp", "fsdp"), None),
        P(("dp", "fsdp")),
        P(("dp", "fsdp")),
        P(("dp", "fsdp"), None),
        P(("dp", "fsdp"), None),
        P(("dp", "fsdp"), None),
        P(("dp", "fsdp"), None),
        P(("dp", "fsdp"), None),
        P(("dp", "fsdp"), None),
        P(("dp", "fsdp"), None),
        P(("dp", "fsdp"), None),
        P(("dp", "fsdp"), None),
        P(("dp", "fsdp"), None),
        P(("dp", "fsdp"), None),
        P(("dp", "fsdp"), None),
        P(("dp", "fsdp")),
        P(("dp", "fsdp")),
        P(("dp", "fsdp")),
    )
    return jax.shard_map(
        per_device,
        mesh=mesh,
        in_specs=placed,
        out_specs=(
            P(("dp", "fsdp"), None),
            P(("dp", "fsdp"), None),
            P(("dp", "fsdp"), None),
            P(("dp", "fsdp"), None),
            P(("dp", "fsdp"), None),
            P(("dp", "fsdp"), None),
            P(("dp", "fsdp"), None),
            P(("dp", "fsdp"), None),
            P(("dp", "fsdp"), None),
            P(("dp", "fsdp"), None),
            P(("dp", "fsdp"), None),
            P(("dp", "fsdp"), None),
            P(("dp", "fsdp"), None),
            P(("dp", "fsdp"), None),
            P(("dp", "fsdp"), None),
            P(("dp", "fsdp"), None),
            P(("dp", "fsdp"), None),
            P(("dp", "fsdp"), None),
            P(("dp", "fsdp"), None),
            P(("dp", "fsdp"), None),
            P(("dp", "fsdp"), None),
            P(("dp", "fsdp"), None),
            P(("dp", "fsdp")),
            P(("dp", "fsdp")),
            P(("dp", "fsdp")),
            P(("dp", "fsdp")),
            P(("dp", "fsdp")),
        ),
        check_vma=False,
    )
```

profile of v0, /device:TPU:0, one launch (start us, length us, event | category | flops | bytes accessed | tf_op | source)
XLA Modules:
  0.0 1735.6 jit_solution(15338248548122503881)
XLA Ops:
  13.3 42.5 %all-reduce = bf16[9216]{0:T(1024)(128)(2,1)S(1)} all-reduce(bf16[9216]{0:T(1024)(128)(2,1)S(1)} %dynamic-update-slice), channel_id=1, replica_groups=mesh['dp'=2,'fsdp'=16] {'dp','fsdp'}, use_global_device_ids=true, to_apply=%add | all-reduce | flops 9216 | bytes 36864
  59.9 14.5 all-gather.5.cloned.1.call-done
  74.3 7.2 fusion.91
  88.1 3.9 copy.91
  96.0 69.7 %while.28 = (s32[]{:T(128)}, bf16[6,1190,2,64]{1,3,2,0:T(8,128)(2,1)}, f32[6,2,1190]{2,1,0:T(2,128)}, bf16[6,1190,2,64]{1,3,2,0:T(8,128)(2,1)}, bf16[6,1190,2,64...) while((s32[]{:T(128)}, ...), condition=%wide.region_5.6_spmd.clone, body=%wide.region_2.5_spmd.clone.sunk | while | flops 752099008 | bytes 38217872 | solution.py:135
  103.1 4.1 fusion.171
  114.7 4.1 fusion.171
  126.3 4.0 fusion.171
  137.9 4.0 fusion.171
  149.4 4.1 fusion.171
  161.0 4.0 fusion.171
  171.9 24.6 %all-gather.9.cloned.1.call-done = bf16[768,3072]{1,0:T(8,128)(2,1)} async-done(((bf16[24,3072]{1,0:T(8,128)(2,1)}), bf16[768,3072]{1,0:T(8,128)(2,1)}) %all-gather.9.cloned.1.call-update) | async-done | bytes 4718608 | tf_op jit(solution)/shard_map/all_gather | solution.py:83
  196.5 42.3 %fusion.77 = (bf16[1190,3072]{1,0:T(8,128)(2,1)S(1)}, f32[1190,3072]{1,0:T(8,128)}) fusion(f32[3072]{0:T(1024)S(1)} %add.185, bf16[768,3072]{1,0:T(8,128)(2,1)} %all-gather.9.cloned.1.call-done, f32[1190,768]{1,0:T(8,128)} %copy-done.3, f32[768]{0:T(1024)S(1)} %get-tuple-element.190, f32[768]{0:T(1024)S(1)} %get-tuple-element.191, ...), kind=kOutput, calls=%fused_computation.70 | convolution fusion | flops 5860968960 | bytes 30336304 | tf_op jit(solution)/shard_map/dot_general | solution.py:144
  241.8 9.5 fusion.111
  251.5 134.6 %reduce-scatter.11.cloned.1.call-done = f32[96,768]{1,0:T(8,128)} async-done(((f32[3072,768]{1,0:T(8,128)}), f32[96,768]{1,0:T(8,128)}) %reduce-scatter.11.cloned.1.call-update) | async-done | bytes 294928 | tf_op jit(solution)/shard_map/reduce_scatter | solution.py:218
  388.1 63.8 %all-gather.11.cloned.1.call-done = bf16[3072,768]{1,0:T(8,128)(2,1)} async-done(((bf16[96,768]{1,0:T(8,128)(2,1)}), bf16[3072,768]{1,0:T(8,128)(2,1)}) %all-gather.11.cloned.1.call-update) | async-done | bytes 4718608 | tf_op jit(solution)/shard_map/all_gather | solution.py:84
  451.9 14.4 convert_reduce_fusion
  466.3 12.8 multiply_reduce_fusion.1
  492.9 961.5 %while.29 = (s32[]{:T(128)}, bf16[6,1190,2,64]{1,3,2,0:T(8,128)(2,1)}, bf16[6,1190,2,64]{1,3,2,0:T(8,128)(2,1)}, bf16[6,1190,2,64]{1,3,2,0:T(8,128)(2,1)}, bf16[...) while((s32[]{:T(128)}, ...), condition=%wide.region_12.13_spmd.clone, body=%wide.region_10.12_spmd.clone.sunk | while | flops 1856815360 | bytes 236936464 | solution.py:184
  495.9 7.3 fusion.183
  503.2 19.9 %copy.130 = f32[2,1190,1190]{2,0,1:T(2,128)} copy(f32[2,1190,1190]{1,2,0:T(8,128)} %fusion.183) | data formatting | bytes 22657600 | tf_op jit(solution)/shard_map/while/body/eval_jaxpr/qhd,khd->hqk/dot_general | solution.py:61
  523.1 7.3 fusion.184
  530.4 19.8 %copy.132 = f32[2,1190,1190]{2,0,1:T(2,128)} copy(f32[2,1190,1190]{1,2,0:T(8,128)} %fusion.184) | data formatting | bytes 22657600 | tf_op jit(solution)/shard_map/while/body/eval_jaxpr/qhd,khd->hqk/dot_general | solution.py:56
  550.2 70.8 %fusion.185 = bf16[2,1190,1190]{2,0,1:T(2,128)(2,1)} fusion(f32[2,1190,1190]{2,0,1:T(2,128)} %copy.130, f32[2,1190]{0,1:T(8,128)S(1)} %bitcast.131, f32[2,1190,1190]{2,0,1:T(2,128)} %copy.132, pred[1190,1190]{1,0:T(8,128)(4,1)S(1)} %compare_and_fusion.5), kind=kOutput, calls=%fused_computation.24.clone.1 | output fusion | flops 28325568 | bytes 29747620 | tf_op jit(solution)/shard_map/while/body/eval_jaxpr/sub | solution.py:68
  621.0 23.7 %fusion.188 = bf16[2,1190,1190]{2,0,1:T(2,128)(2,1)S(1)} fusion(f32[2,1190]{0,1:T(8,128)S(1)} %bitcast.132, f32[2,1190,1190]{2,0,1:T(2,128)S(1)} %copy-done, pred[1190,1190]{1,0:T(8,128)(4,1)S(1)} %compare_and_fusion.5), kind=kLoop, calls=%fused_computation.65.clone.1 | loop fusion | flops 11328800 | bytes 18418820 | tf_op jit(solution)/shard_map/while/body/eval_jaxpr/convert_element_type | solution.py:60
  656.1 7.3 fusion.183
  663.4 19.8 %copy.130 = f32[2,1190,1190]{2,0,1:T(2,128)} copy(f32[2,1190,1190]{1,2,0:T(8,128)} %fusion.183) | data formatting | bytes 22657600 | tf_op jit(solution)/shard_map/while/body/eval_jaxpr/qhd,khd->hqk/dot_general | solution.py:61
  683.2 7.3 fusion.184
  690.6 19.7 %copy.132 = f32[2,1190,1190]{2,0,1:T(2,128)} copy(f32[2,1190,1190]{1,2,0:T(8,128)} %fusion.184) | data formatting | bytes 22657600 | tf_op jit(solution)/shard_map/while/body/eval_jaxpr/qhd,khd->hqk/dot_general | solution.py:56
  710.3 70.8 %fusion.185 = bf16[2,1190,1190]{2,0,1:T(2,128)(2,1)} fusion(f32[2,1190,1190]{2,0,1:T(2,128)} %copy.130, f32[2,1190]{0,1:T(8,128)S(1)} %bitcast.131, f32[2,1190,1190]{2,0,1:T(2,128)} %copy.132, pred[1190,1190]{1,0:T(8,128)(4,1)S(1)} %compare_and_fusion.5), kind=kOutput, calls=%fused_computation.24.clone.1 | output fusion | flops 28325568 | bytes 29747620 | tf_op jit(solution)/shard_map/while/body/eval_jaxpr/sub | solution.py:68
  781.1 23.7 %fusion.188 = bf16[2,1190,1190]{2,0,1:T(2,128)(2,1)S(1)} fusion(f32[2,1190]{0,1:T(8,128)S(1)} %bitcast.132, f32[2,1190,1190]{2,0,1:T(2,128)S(1)} %copy-done, pred[1190,1190]{1,0:T(8,128)(4,1)S(1)} %compare_and_fusion.5), kind=kLoop, calls=%fused_computation.65.clone.1 | loop fusion | flops 11328800 | bytes 18418820 | tf_op jit(solution)/shard_map/while/body/eval_jaxpr/convert_element_type | solution.py:60
  816.2 7.3 fusion.183
  823.6 19.8 %copy.130 = f32[2,1190,1190]{2,0,1:T(2,128)} copy(f32[2,1190,1190]{1,2,0:T(8,128)} %fusion.183) | data formatting | bytes 22657600 | tf_op jit(solution)/shard_map/while/body/eval_jaxpr/qhd,khd->hqk/dot_general | solution.py:61
  843.4 7.3 fusion.184
  850.7 19.7 %copy.132 = f32[2,1190,1190]{2,0,1:T(2,128)} copy(f32[2,1190,1190]{1,2,0:T(8,128)} %fusion.184) | data formatting | bytes 22657600 | tf_op jit(solution)/shard_map/while/body/eval_jaxpr/qhd,khd->hqk/dot_general | solution.py:56
  870.4 70.8 %fusion.185 = bf16[2,1190,1190]{2,0,1:T(2,128)(2,1)} fusion(f32[2,1190,1190]{2,0,1:T(2,128)} %copy.130, f32[2,1190]{0,1:T(8,128)S(1)} %bitcast.131, f32[2,1190,1190]{2,0,1:T(2,128)} %copy.132, pred[1190,1190]{1,0:T(8,128)(4,1)S(1)} %compare_and_fusion.5), kind=kOutput, calls=%fused_computation.24.clone.1 | output fusion | flops 28325568 | bytes 29747620 | tf_op jit(solution)/shard_map/while/body/eval_jaxpr/sub | solution.py:68
  941.2 23.7 %fusion.188 = bf16[2,1190,1190]{2,0,1:T(2,128)(2,1)S(1)} fusion(f32[2,1190]{0,1:T(8,128)S(1)} %bitcast.132, f32[2,1190,1190]{2,0,1:T(2,128)S(1)} %copy-done, pred[1190,1190]{1,0:T(8,128)(4,1)S(1)} %compare_and_fusion.5), kind=kLoop, calls=%fused_computation.65.clone.1 | loop fusion | flops 11328800 | bytes 18418820 | tf_op jit(solution)/shard_map/while/body/eval_jaxpr/convert_element_type | solution.py:60
  976.4 7.3 fusion.183
  983.7 19.8 %copy.130 = f32[2,1190,1190]{2,0,1:T(2,128)} copy(f32[2,1190,1190]{1,2,0:T(8,128)} %fusion.183) | data formatting | bytes 22657600 | tf_op jit(solution)/shard_map/while/body/eval_jaxpr/qhd,khd->hqk/dot_general | solution.py:61
  1003.5 7.3 fusion.184
  1010.8 19.7 %copy.132 = f32[2,1190,1190]{2,0,1:T(2,128)} copy(f32[2,1190,1190]{1,2,0:T(8,128)} %fusion.184) | data formatting | bytes 22657600 | tf_op jit(solution)/shard_map/while/body/eval_jaxpr/qhd,khd->hqk/dot_general | solution.py:56
  1030.6 70.8 %fusion.185 = bf16[2,1190,1190]{2,0,1:T(2,128)(2,1)} fusion(f32[2,1190,1190]{2,0,1:T(2,128)} %copy.130, f32[2,1190]{0,1:T(8,128)S(1)} %bitcast.131, f32[2,1190,1190]{2,0,1:T(2,128)} %copy.132, pred[1190,1190]{1,0:T(8,128)(4,1)S(1)} %compare_and_fusion.5), kind=kOutput, calls=%fused_computation.24.clone.1 | output fusion | flops 28325568 | bytes 29747620 | tf_op jit(solution)/shard_map/while/body/eval_jaxpr/sub | solution.py:68
  1101.4 23.7 %fusion.188 = bf16[2,1190,1190]{2,0,1:T(2,128)(2,1)S(1)} fusion(f32[2,1190]{0,1:T(8,128)S(1)} %bitcast.132, f32[2,1190,1190]{2,0,1:T(2,128)S(1)} %copy-done, pred[1190,1190]{1,0:T(8,128)(4,1)S(1)} %compare_and_fusion.5), kind=kLoop, calls=%fused_computation.65.clone.1 | loop fusion | flops 11328800 | bytes 18418820 | tf_op jit(solution)/shard_map/while/body/eval_jaxpr/convert_element_type | solution.py:60
  1136.5 7.3 fusion.183
  1143.8 19.8 %copy.130 = f32[2,1190,1190]{2,0,1:T(2,128)} copy(f32[2,1190,1190]{1,2,0:T(8,128)} %fusion.183) | data formatting | bytes 22657600 | tf_op jit(solution)/shard_map/while/body/eval_jaxpr/qhd,khd->hqk/dot_general | solution.py:61
  1163.6 7.3 fusion.184
  1171.0 19.7 %copy.132 = f32[2,1190,1190]{2,0,1:T(2,128)} copy(f32[2,1190,1190]{1,2,0:T(8,128)} %fusion.184) | data formatting | bytes 22657600 | tf_op jit(solution)/shard_map/while/body/eval_jaxpr/qhd,khd->hqk/dot_general | solution.py:56
  1190.7 70.8 %fusion.185 = bf16[2,1190,1190]{2,0,1:T(2,128)(2,1)} fusion(f32[2,1190,1190]{2,0,1:T(2,128)} %copy.130, f32[2,1190]{0,1:T(8,128)S(1)} %bitcast.131, f32[2,1190,1190]{2,0,1:T(2,128)} %copy.132, pred[1190,1190]{1,0:T(8,128)(4,1)S(1)} %compare_and_fusion.5), kind=kOutput, calls=%fused_computation.24.clone.1 | output fusion | flops 28325568 | bytes 29747620 | tf_op jit(solution)/shard_map/while/body/eval_jaxpr/sub | solution.py:68
  1261.5 23.7 %fusion.188 = bf16[2,1190,1190]{2,0,1:T(2,128)(2,1)S(1)} fusion(f32[2,1190]{0,1:T(8,128)S(1)} %bitcast.132, f32[2,1190,1190]{2,0,1:T(2,128)S(1)} %copy-done, pred[1190,1190]{1,0:T(8,128)(4,1)S(1)} %compare_and_fusion.5), kind=kLoop, calls=%fused_computation.65.clone.1 | loop fusion | flops 11328800 | bytes 18418820 | tf_op jit(solution)/shard_map/while/body/eval_jaxpr/convert_element_type | solution.py:60
  1296.6 7.3 fusion.183
  1304.0 19.8 %copy.130 = f32[2,1190,1190]{2,0,1:T(2,128)} copy(f32[2,1190,1190]{1,2,0:T(8,128)} %fusion.183) | data formatting | bytes 22657600 | tf_op jit(solution)/shard_map/while/body/eval_jaxpr/qhd,khd->hqk/dot_general | solution.py:61
  1323.8 7.3 fusion.184
  1331.1 19.7 %copy.132 = f32[2,1190,1190]{2,0,1:T(2,128)} copy(f32[2,1190,1190]{1,2,0:T(8,128)} %fusion.184) | data formatting | bytes 22657600 | tf_op jit(solution)/shard_map/while/body/eval_jaxpr/qhd,khd->hqk/dot_general | solution.py:56
  1350.8 70.8 %fusion.185 = bf16[2,1190,1190]{2,0,1:T(2,128)(2,1)} fusion(f32[2,1190,1190]{2,0,1:T(2,128)} %copy.130, f32[2,1190]{0,1:T(8,128)S(1)} %bitcast.131, f32[2,1190,1190]{2,0,1:T(2,128)} %copy.132, pred[1190,1190]{1,0:T(8,128)(4,1)S(1)} %compare_and_fusion.5), kind=kOutput, calls=%fused_computation.24.clone.1 | output fusion | flops 28325568 | bytes 29747620 | tf_op jit(solution)/shard_map/while/body/eval_jaxpr/sub | solution.py:68
  1421.6 23.7 %fusion.188 = bf16[2,1190,1190]{2,0,1:T(2,128)(2,1)S(1)} fusion(f32[2,1190]{0,1:T(8,128)S(1)} %bitcast.132, f32[2,1190,1190]{2,0,1:T(2,128)S(1)} %copy-done, pred[1190,1190]{1,0:T(8,128)(4,1)S(1)} %compare_and_fusion.5), kind=kLoop, calls=%fused_computation.65.clone.1 | loop fusion | flops 11328800 | bytes 18418820 | tf_op jit(solution)/shard_map/while/body/eval_jaxpr/convert_element_type | solution.py:60
  1454.4 11.6 fusion.117
  1466.7 12.8 fusion.121
  1481.5 4.0 convert_reduce_fusion.1
  1485.7 10.8 fusion.106
  1497.0 40.0 %all-reduce.1 = f32[9216]{0:T(1024)S(1)} all-reduce(f32[9216]{0:T(1024)S(1)} %reshape.182), channel_id=6, replica_groups=mesh['dp'=2,'fsdp'=16] {'dp','fsdp'}, use_global_device_ids=true, to_apply=%region_27.28.clone | all-reduce | flops 9216 | bytes 73728
  1538.3 5.2 fusion.105
  1543.6 10.6 fusion.110
  1556.6 27.7 %reduce-scatter.5.cloned.1.call-done = f32[24,2304]{1,0:T(8,128)} async-done(((f32[768,2304]{1,0:T(8,128)}), f32[24,2304]{1,0:T(8,128)}) %reduce-scatter.5.cloned.1.call-update) | async-done | bytes 221200 | tf_op jit(solution)/shard_map/reduce_scatter | solution.py:215
  1586.7 139.2 %reduce-scatter.9.cloned.1.call-done = f32[24,3072]{1,0:T(8,128)} async-done(((f32[768,3072]{1,0:T(8,128)}), f32[24,3072]{1,0:T(8,128)}) %reduce-scatter.9.cloned.1.call-update) | async-done | bytes 294928 | tf_op jit(solution)/shard_map/reduce_scatter | solution.py:217
  (330 shorter events, 170.7 us)
Async XLA Ops:
  7.2 50.8 %copy-start.7 = (s32[1190]{0:T(1024)S(1)}, s32[1190]{0:T(1024)}, u32[]{:S(2)}) copy-start(s32[1190]{0:T(1024)} %param.26) | copy-start | bytes 14284
  7.2 51.4 %copy-start.1 = (bf16[1190,768]{1,0:T(8,128)(2,1)S(1)}, bf16[1190,768]{1,0:T(8,128)(2,1)}, u32[]{:S(2)}) copy-start(bf16[1190,768]{1,0:T(8,128)(2,1)} %param.23) | copy-start | bytes 5483524
  7.2 67.1 %all-gather.5.cloned.1.call-start = ((), (), s32[]{:S(2)}) async-start(), calls=%async_computation.4 | async-start | bytes 3649536 | tf_op jit(solution)/shard_map/all_gather | solution.py:81
  9.0 156.6 %all-gather.7.cloned.1.call-start = ((), (), s32[]{:S(2)}) async-start(), calls=%async_computation.5 | async-start | bytes 1216512 | tf_op jit(solution)/shard_map/all_gather | solution.py:82
  10.6 185.9 %all-gather.9.cloned.1.call-start = ((), (), s32[]{:S(2)}) async-start(), calls=%async_computation.6 | async-start | bytes 4866048 | tf_op jit(solution)/shard_map/all_gather | solution.py:83
  12.3 373.8 %reduce-scatter.11.cloned.1.call-start = ((), (), s32[]{:S(2)}) async-start(), calls=%async_computation.11 | async-start | bytes 9732096 | tf_op jit(solution)/shard_map/reduce_scatter | solution.py:218
  57.8 23.8 %copy-start.43 = (f32[768]{0:T(1024)}, f32[768]{0:T(1024)S(1)}, u32[]{:S(2)}) copy-start(f32[768]{0:T(1024)S(1)} %get-tuple-element.196) | copy-start | bytes 9220
  57.8 23.8 %copy-start.55 = (f32[768]{0:T(1024)}, f32[768]{0:T(1024)S(1)}, u32[]{:S(2)}) copy-start(f32[768]{0:T(1024)S(1)} %get-tuple-element.195) | copy-start | bytes 9220
  57.8 138.7 %copy-start.53 = (f32[768]{0:T(1024)}, f32[768]{0:T(1024)S(1)}, u32[]{:S(2)}) copy-start(f32[768]{0:T(1024)S(1)} %get-tuple-element.190) | copy-start | bytes 9220
  57.8 421.3 %copy-start.45 = (f32[768]{0:T(1024)}, f32[768]{0:T(1024)S(1)}, u32[]{:S(2)}) copy-start(f32[768]{0:T(1024)S(1)} %get-tuple-element.191) | copy-start | bytes 9220
  59.0 22.6 %copy-start.34 = (f32[1190]{0:T(1024)}, f32[1190]{0:T(1024)S(1)}, u32[]{:S(2)}) copy-start(f32[1190]{0:T(1024)S(1)} %broadcast_multiply_fusion.5) | copy-start | bytes 14284
  59.7 21.9 %copy-start.38 = (f32[1190]{0:T(1024)}, f32[1190]{0:T(1024)S(1)}, u32[]{:S(2)}) copy-start(f32[1190]{0:T(1024)S(1)} %add_rsqrt_fusion.1) | copy-start | bytes 14284
  88.1 7.9 copy-start.9
  169.5 309.7 %copy-start.36 = (f32[1190]{0:T(1024)}, f32[1190]{0:T(1024)S(1)}, u32[]{:S(2)}) copy-start(f32[1190]{0:T(1024)S(1)} %broadcast_multiply_fusion.4) | copy-start | bytes 14284
  171.9 307.3 %copy-start.40 = (f32[1190]{0:T(1024)}, f32[1190]{0:T(1024)S(1)}, u32[]{:S(2)}) copy-start(f32[1190]{0:T(1024)S(1)} %add_rsqrt_fusion) | copy-start | bytes 14284
  196.5 45.3 %copy-start.17 = (bf16[1190,768]{1,0:T(8,128)(2,1)S(1)}, bf16[1190,768]{1,0:T(8,128)(2,1)}, u32[]{:S(2)}) copy-start(bf16[1190,768]{1,0:T(8,128)(2,1)} %param.24) | copy-start | bytes 5483524
  196.5 45.3 %copy-start.42 = (f32[1190]{0:T(1024)S(1)}, f32[1190]{0:T(1024)}, u32[]{:S(2)}) copy-start(f32[1190]{0:T(1024)} %convert_element_type.106) | copy-start | bytes 14284
  251.4 134.7 %copy-start.23 = (f32[96,768]{1,0:T(8,128)S(1)}, f32[96,768]{1,0:T(8,128)}, u32[]{:S(2)}) copy-start(f32[96,768]{1,0:T(8,128)} %param.36) | copy-start | bytes 884740
  251.4 134.7 %copy-start.24 = (f32[96,768]{1,0:T(8,128)S(1)}, f32[96,768]{1,0:T(8,128)}, u32[]{:S(2)}) copy-start(f32[96,768]{1,0:T(8,128)} %param.37) | copy-start | bytes 884740
  251.4 200.4 %all-gather.11.cloned.1.call-start = ((), (), s32[]{:S(2)}) async-start(), calls=%async_computation.7 | async-start | bytes 4866048 | tf_op jit(solution)/shard_map/all_gather | solution.py:84
  388.0 1166.3 %reduce-scatter.7.cloned.1.call-start = ((), (), s32[]{:S(2)}) async-start(), calls=%async_computation.9 | async-start | bytes 2433024 | tf_op jit(solution)/shard_map/reduce_scatter | solution.py:216
  451.9 14.5 copy-start.4
  466.3 12.8 copy-start.64
  486.8 1097.5 %reduce-scatter.5.cloned.1.call-start = ((), (), s32[]{:S(2)}) async-start(), calls=%async_computation.8 | async-start | bytes 7299072 | tf_op jit(solution)/shard_map/reduce_scatter | solution.py:215
  492.8 961.5 %copy-start.35 = (f32[1190]{0:T(1024)S(1)}, f32[1190]{0:T(1024)}, u32[]{:S(2)}) copy-start(f32[1190]{0:T(1024)} %copy-done.34) | copy-start | bytes 14284
  492.9 961.5 %copy-start.39 = (f32[1190]{0:T(1024)S(1)}, f32[1190]{0:T(1024)}, u32[]{:S(2)}) copy-start(f32[1190]{0:T(1024)} %copy-done.38) | copy-start | bytes 14284
  492.9 961.5 %copy-start.44 = (f32[768]{0:T(1024)S(1)}, f32[768]{0:T(1024)}, u32[]{:S(2)}) copy-start(f32[768]{0:T(1024)} %copy-done.43) | copy-start | bytes 9220
  492.9 961.5 %copy-start.56 = (f32[768]{0:T(1024)S(1)}, f32[768]{0:T(1024)}, u32[]{:S(2)}) copy-start(f32[768]{0:T(1024)} %copy-done.55) | copy-start | bytes 9220
  550.2 70.8 %copy-start = (f32[2,1190,1190]{2,0,1:T(2,128)S(1)}, f32[2,1190,1190]{2,0,1:T(2,128)}, u32[]{:S(2)}) copy-start(f32[2,1190,1190]{2,0,1:T(2,128)} %copy.132) | copy-start | bytes 33986404 | tf_op jit(solution)/shard_map/while
  621.0 23.7 %copy-start.11 = (bf16[6,1190,2,64]{1,3,2,0:T(8,128)(2,1)S(1)}, bf16[6,1190,2,64]{1,3,2,0:T(8,128)(2,1)}, u32[]{:S(2)}) copy-start(bf16[6,1190,2,64]{1,3,2,0:T(8,128)(2,1)} %get-tuple-element.434) | copy-start | bytes 5483524 | tf_op jit(solution)/shard_map/while
  621.0 26.2 %copy-start.63 = (bf16[2,1190,1190]{2,0,1:T(2,128)(2,1)S(1)}, bf16[2,1190,1190]{2,0,1:T(2,128)(2,1)}, u32[]{:S(2)}) copy-start(bf16[2,1190,1190]{2,0,1:T(2,128)(2,1)} %fusion.185) | copy-start | bytes 16993204 | tf_op jit(solution)/shard_map/while
  710.3 70.8 %copy-start = (f32[2,1190,1190]{2,0,1:T(2,128)S(1)}, f32[2,1190,1190]{2,0,1:T(2,128)}, u32[]{:S(2)}) copy-start(f32[2,1190,1190]{2,0,1:T(2,128)} %copy.132) | copy-start | bytes 33986404 | tf_op jit(solution)/shard_map/while
  781.1 23.7 %copy-start.11 = (bf16[6,1190,2,64]{1,3,2,0:T(8,128)(2,1)S(1)}, bf16[6,1190,2,64]{1,3,2,0:T(8,128)(2,1)}, u32[]{:S(2)}) copy-start(bf16[6,1190,2,64]{1,3,2,0:T(8,128)(2,1)} %get-tuple-element.434) | copy-start | bytes 5483524 | tf_op jit(solution)/shard_map/while
  781.1 26.2 %copy-start.63 = (bf16[2,1190,1190]{2,0,1:T(2,128)(2,1)S(1)}, bf16[2,1190,1190]{2,0,1:T(2,128)(2,1)}, u32[]{:S(2)}) copy-start(bf16[2,1190,1190]{2,0,1:T(2,128)(2,1)} %fusion.185) | copy-start | bytes 16993204 | tf_op jit(solution)/shard_map/while
  870.4 70.8 %copy-start = (f32[2,1190,1190]{2,0,1:T(2,128)S(1)}, f32[2,1190,1190]{2,0,1:T(2,128)}, u32[]{:S(2)}) copy-start(f32[2,1190,1190]{2,0,1:T(2,128)} %copy.132) | copy-start | bytes 33986404 | tf_op jit(solution)/shard_map/while
  941.2 23.7 %copy-start.11 = (bf16[6,1190,2,64]{1,3,2,0:T(8,128)(2,1)S(1)}, bf16[6,1190,2,64]{1,3,2,0:T(8,128)(2,1)}, u32[]{:S(2)}) copy-start(bf16[6,1190,2,64]{1,3,2,0:T(8,128)(2,1)} %get-tuple-element.434) | copy-start | bytes 5483524 | tf_op jit(solution)/shard_map/while
  941.2 26.2 %copy-start.63 = (bf16[2,1190,1190]{2,0,1:T(2,128)(2,1)S(1)}, bf16[2,1190,1190]{2,0,1:T(2,128)(2,1)}, u32[]{:S(2)}) copy-start(bf16[2,1190,1190]{2,0,1:T(2,128)(2,1)} %fusion.185) | copy-start | bytes 16993204 | tf_op jit(solution)/shard_map/while
  1030.6 70.8 %copy-start = (f32[2,1190,1190]{2,0,1:T(2,128)S(1)}, f32[2,1190,1190]{2,0,1:T(2,128)}, u32[]{:S(2)}) copy-start(f32[2,1190,1190]{2,0,1:T(2,128)} %copy.132) | copy-start | bytes 33986404 | tf_op jit(solution)/shard_map/while
  1101.3 23.7 %copy-start.11 = (bf16[6,1190,2,64]{1,3,2,0:T(8,128)(2,1)S(1)}, bf16[6,1190,2,64]{1,3,2,0:T(8,128)(2,1)}, u32[]{:S(2)}) copy-start(bf16[6,1190,2,64]{1,3,2,0:T(8,128)(2,1)} %get-tuple-element.434) | copy-start | bytes 5483524 | tf_op jit(solution)/shard_map/while
  1101.4 26.2 %copy-start.63 = (bf16[2,1190,1190]{2,0,1:T(2,128)(2,1)S(1)}, bf16[2,1190,1190]{2,0,1:T(2,128)(2,1)}, u32[]{:S(2)}) copy-start(bf16[2,1190,1190]{2,0,1:T(2,128)(2,1)} %fusion.185) | copy-start | bytes 16993204 | tf_op jit(solution)/shard_map/while
  1190.7 70.8 %copy-start = (f32[2,1190,1190]{2,0,1:T(2,128)S(1)}, f32[2,1190,1190]{2,0,1:T(2,128)}, u32[]{:S(2)}) copy-start(f32[2,1190,1190]{2,0,1:T(2,128)} %copy.132) | copy-start | bytes 33986404 | tf_op jit(solution)/shard_map/while
  1261.5 23.7 %copy-start.11 = (bf16[6,1190,2,64]{1,3,2,0:T(8,128)(2,1)S(1)}, bf16[6,1190,2,64]{1,3,2,0:T(8,128)(2,1)}, u32[]{:S(2)}) copy-start(bf16[6,1190,2,64]{1,3,2,0:T(8,128)(2,1)} %get-tuple-element.434) | copy-start | bytes 5483524 | tf_op jit(solution)/shard_map/while
  1261.5 26.2 %copy-start.63 = (bf16[2,1190,1190]{2,0,1:T(2,128)(2,1)S(1)}, bf16[2,1190,1190]{2,0,1:T(2,128)(2,1)}, u32[]{:S(2)}) copy-start(bf16[2,1190,1190]{2,0,1:T(2,128)(2,1)} %fusion.185) | copy-start | bytes 16993204 | tf_op jit(solution)/shard_map/while
  1350.8 70.8 %copy-start = (f32[2,1190,1190]{2,0,1:T(2,128)S(1)}, f32[2,1190,1190]{2,0,1:T(2,128)}, u32[]{:S(2)}) copy-start(f32[2,1190,1190]{2,0,1:T(2,128)} %copy.132) | copy-start | bytes 33986404 | tf_op jit(solution)/shard_map/while
  1421.6 23.7 %copy-start.11 = (bf16[6,1190,2,64]{1,3,2,0:T(8,128)(2,1)S(1)}, bf16[6,1190,2,64]{1,3,2,0:T(8,128)(2,1)}, u32[]{:S(2)}) copy-start(bf16[6,1190,2,64]{1,3,2,0:T(8,128)(2,1)} %get-tuple-element.434) | copy-start | bytes 5483524 | tf_op jit(solution)/shard_map/while
  1421.6 26.2 %copy-start.63 = (bf16[2,1190,1190]{2,0,1:T(2,128)(2,1)S(1)}, bf16[2,1190,1190]{2,0,1:T(2,128)(2,1)}, u32[]{:S(2)}) copy-start(bf16[2,1190,1190]{2,0,1:T(2,128)(2,1)} %fusion.185) | copy-start | bytes 16993204 | tf_op jit(solution)/shard_map/while
  1466.0 259.9 %reduce-scatter.9.cloned.1.call-start = ((), (), s32[]{:S(2)}) async-start(), calls=%async_computation.10 | async-start | bytes 9732096 | tf_op jit(solution)/shard_map/reduce_scatter | solution.py:217
  1479.7 5.9 copy-start.2
  1485.6 51.4 %copy-start.51 = (f32[288]{0:T(512)S(1)}, f32[288]{0:T(512)}, u32[]{:S(2)}) copy-start(f32[288]{0:T(512)} %param.39) | copy-start | bytes 3460
  1485.7 51.4 %copy-start.59 = (f32[288]{0:T(512)S(1)}, f32[288]{0:T(512)}, u32[]{:S(2)}) copy-start(f32[288]{0:T(512)} %param.40) | copy-start | bytes 3460
  1485.7 52.1 %copy-start.60 = (f32[288]{0:T(512)S(1)}, f32[288]{0:T(512)}, u32[]{:S(2)}) copy-start(f32[288]{0:T(512)} %param.41) | copy-start | bytes 3460
  1537.7 5.8 copy-start.50
  1538.3 5.2 copy-start.52
  1543.5 10.7 copy-start.29
  1543.6 10.7 copy-start.32
  1543.6 12.3 copy-start.33
  1543.6 40.7 %copy-start.21 = (f32[24,2304]{1,0:T(8,128)S(1)}, f32[24,2304]{1,0:T(8,128)}, u32[]{:S(2)}) copy-start(f32[24,2304]{1,0:T(8,128)} %param.27) | copy-start | bytes 663556
  1543.6 40.6 %copy-start.30 = (f32[24,2304]{1,0:T(8,128)S(1)}, f32[24,2304]{1,0:T(8,128)}, u32[]{:S(2)}) copy-start(f32[24,2304]{1,0:T(8,128)} %param.28) | copy-start | bytes 663556
  1543.6 42.4 %copy-start.31 = (f32[24,2304]{1,0:T(8,128)S(1)}, f32[24,2304]{1,0:T(8,128)}, u32[]{:S(2)}) copy-start(f32[24,2304]{1,0:T(8,128)} %param.29) | copy-start | bytes 663556
  1543.6 182.3 %copy-start.20 = (f32[24,3072]{1,0:T(8,128)S(1)}, f32[24,3072]{1,0:T(8,128)}, u32[]{:S(2)}) copy-start(f32[24,3072]{1,0:T(8,128)} %param.33) | copy-start | bytes 884740
  1543.6 182.3 %copy-start.26 = (f32[24,3072]{1,0:T(8,128)S(1)}, f32[24,3072]{1,0:T(8,128)}, u32[]{:S(2)}) copy-start(f32[24,3072]{1,0:T(8,128)} %param.34) | copy-start | bytes 884740
  1554.3 173.4 %copy-start.27 = (f32[24,3072]{1,0:T(8,128)S(1)}, f32[24,3072]{1,0:T(8,128)}, u32[]{:S(2)}) copy-start(f32[24,3072]{1,0:T(8,128)} %param.35) | copy-start | bytes 884740
  1555.9 172.6 %copy-start.28 = (f32[24,768]{1,0:T(8,128)}, f32[24,768]{1,0:T(8,128)S(1)}, u32[]{:S(2)}) copy-start(f32[24,768]{1,0:T(8,128)S(1)} %get-tuple-element.248) | copy-start | bytes 221188
  1586.0 142.6 %copy-start.22 = (f32[24,2304]{1,0:T(8,128)}, f32[24,2304]{1,0:T(8,128)S(1)}, u32[]{:S(2)}) copy-start(f32[24,2304]{1,0:T(8,128)S(1)} %get-tuple-element.251) | copy-start | bytes 663556
  (40 other events, 100.9 us)
Sparse Core Ops, SparseCore 0:
  11.5 62.7 all-gather.4
  77.8 52.7 all-gather.6
  134.0 62.4 all-gather.8
  251.5 134.4 reduce-scatter.10
  389.4 62.4 all-gather.10
  486.9 98.2 reduce-scatter.6
  1466.2 118.0 reduce-scatter.4
  1590.7 135.1 reduce-scatter.8
where the time goes:
time: 1750 us; the launch traced here: 1740 us
  other arithmetic  630 us (36%)
  waiting for transfers between devices  404 us (23%)
  matrix products  330 us (19%)
  local copies, waits for them, and re-layouts  272 us (16%)
  blocking collectives  82.5 us (5%)
    sub x6, other arithmetic, pair_backward(): score_grad = (probs * (prob_grad - row_terms)).astype(jnp.bfloat16)  424 us
    convert_element_type x6, other arithmetic, pair_backward(): weights = probs.astype(jnp.bfloat16)  142 us
    reduce_scatter x1, waiting for transfers between devices, per_device(): lax.psum_scatter(expand_part, ('dp', 'fsdp'), scatter_dimension=0, tiled=...  139 us
    reduce_scatter x1, waiting for transfers between devices, per_device(): lax.psum_scatter(shrink_part, ('dp', 'fsdp'), scatter_dimension=0, tiled=...  135 us
    dot_general x6, local copies, waits for them, and re-layouts, pair_backward(): jnp.einsum('qhd,khd->hqk', upstream_pair, value_pair, preferred_element_t...  119 us
    dot_general x6, local copies, waits for them, and re-layouts, pair_backward(): jnp.einsum('qhd,khd->hqk', query_pair, key_pair, preferred_element_type=j...  118 us
    unnamed x2, blocking collectives  82.5 us
    all_gather x1, waiting for transfers between devices, gather_all(): lax.all_gather(shrink_piece, ('dp', 'fsdp'), axis=0, tiled=True)  63.8 us
  transfers between devices with their start and end apart: 8, of which 6 were waited for; matrix products, arithmetic and copies ran while one was open for 65% of the time, Pallas kernels for 0%

commit v1 on v0

v1 whole, which is shorter than its diff:
```python
from functools import partial
import jax, jax.numpy as jnp
from jax import lax
from jax.sharding import PartitionSpec as P
from jax.experimental import pallas as pl
from jax.experimental.pallas import tpu as pltpu

HEAD_DIM = 64
BIG = 2.0 ** 100
F32 = jnp.float32
BF16 = jnp.bfloat16


def round_up(n, m):
    return (n + m - 1) // m * m


def mask_features(segments, padding, slots):
    wide = round_up(slots, 256)
    group = segments * 2 + padding
    group = jnp.concatenate([group, jnp.full((wide - slots,), 4, jnp.int32)])[:, None]
    lane = lax.broadcasted_iota(jnp.int32, (wide, 128), 1) % HEAD_DIM
    same = group == lane
    query_side = jnp.where((lane < 5) & ~same, -BIG, 0.0).astype(BF16)
    key_side = jnp.where(same | ((lane >= 5) & (lane < 8)), 1.0, 0.0).astype(BF16)
    return query_side, key_side


def dot_nt(a, b):
    return lax.dot_general(a, b, (((1,), (1,)), ((), ())), preferred_element_type=F32)


def dot_nn(a, b):
    return lax.dot_general(a, b, (((1,), (0,)), ((), ())), preferred_element_type=F32)


def dot_tn(a, b):
    return lax.dot_general(a, b, (((0,), (0,)), ((), ())), preferred_element_type=F32)


def fill(target, value, features, keep_low, slots):
    wide = target.shape[0]
    start = slots // 16 * 16
    low_half = lax.broadcasted_iota(jnp.int32, (wide - start, 128), 1) < HEAD_DIM
    tail = features[start:wide, :] if features is not None else jnp.ones((wide - start, 128), BF16)
    target[start:wide, :] = jnp.where(low_half == keep_low, jnp.zeros_like(tail), tail)
    target[0:slots, :] = value


def forward_kernel(slots, block, q_ref, k_ref, v_ref, fq_ref, fk_ref,
                   low_ref, wide_ref, lse_ref, qa, qb, ka, kb, va, vb, out, lse):
    low_half = lax.broadcasted_iota(jnp.int32, (slots, 128), 1) < HEAD_DIM
    q = q_ref[...] * 0.125
    fq = fq_ref[0:slots, :]
    fk = fk_ref[0:slots, :]
    fill(qa, jnp.where(low_half, q, fq), fq_ref, True, slots)
    fill(qb, jnp.where(low_half, fq, q), fq_ref, False, slots)
    k = k_ref[...]
    fill(ka, jnp.where(low_half, k, fk), fk_ref, True, slots)
    fill(kb, jnp.where(low_half, fk, k), fk_ref, False, slots)
    v = v_ref[...]
    one = jnp.ones_like(v)
    fill(va, jnp.where(low_half, v, one), None, True, slots)
    fill(vb, jnp.where(low_half, one, v), None, False, slots)
    half = lax.broadcasted_iota(jnp.int32, (block, 128), 1) < HEAD_DIM

    def head(qx, kx, vx, rows):
        scores = dot_nt(qx[rows, :], kx[...])
        top = jnp.max(scores, axis=1, keepdims=True)
        weights = jnp.exp(scores - top).astype(BF16)
        return dot_nn(weights, vx[...]), top

    def step(number, carry):
        rows = pl.ds(pl.multiple_of(number * block, 16), block)
        raw_a, top_a = head(qa, ka, va, rows)
        raw_b, top_b = head(qb, kb, vb, rows)
        sums = jnp.where(half, raw_b, raw_a)
        lse[rows, :] = jnp.where(half, top_b, top_a) + jnp.log(sums)
        out[rows, :] = jnp.where(half, raw_a, raw_b) / pltpu.roll(sums, HEAD_DIM, 1)
        return carry

    lax.fori_loop(0, out.shape[0] // block, step, 0)
    attended = out[0:slots, :]
    low_ref[...] = attended.astype(BF16)
    wide_ref[...] = attended
    lse_ref[...] = lse[0:slots, :]


def column(shift, slots):
    return pl.BlockSpec((slots, 128), lambda p, s=shift: (0, s + p))


def attention_forward(qkv, fq, fk, block=240):
    slots = qkv.shape[0]
    pairs = qkv.shape[1] // 384
    wide = fq.shape[0]
    rows = round_up(slots, block)
    whole = pl.BlockSpec((wide, 128), lambda p: (0, 0))
    width = pairs * 128
    return pl.pallas_call(
        partial(forward_kernel, slots, block),
        grid=(pairs,),
        in_specs=[column(0, slots), column(pairs, slots), column(2 * pairs, slots), whole, whole],
        out_specs=[column(0, slots)] * 3,
        out_shape=[
            jax.ShapeDtypeStruct((slots, width), BF16),
            jax.ShapeDtypeStruct((slots, width), F32),
            jax.ShapeDtypeStruct((slots, width), F32),
        ],
        scratch_shapes=[pltpu.VMEM((wide, 128), BF16)] * 6 + [pltpu.VMEM((rows, 128), F32)] * 2,
        compiler_params=pltpu.CompilerParams(vmem_limit_bytes=50 * 2 ** 20),
        name="attention_forward",
    )(qkv, qkv, qkv, fq, fk)


def thirds(value):
    high = value.astype(BF16)
    rest = value - high.astype(F32)
    mid = rest.astype(BF16)
    return high, mid, (rest - mid.astype(F32)).astype(BF16)


def backward_kernel(slots, block, q_ref, k_ref, v_ref, g_ref, wide_ref, lse_ref, fq_ref, fk_ref,
                    dq_ref, dk_ref, dv_ref, qa, qb, ka, kb, va, vb, ga, gb, dqa, dqb, dk, dv):
    lane = lax.broadcasted_iota(jnp.int32, (slots, 128), 1)
    low_half = lane < HEAD_DIM
    spot = lane % HEAD_DIM
    q = q_ref[...] * 0.125
    fk = fk_ref[0:slots, :]
    high, mid, low = thirds(-lse_ref[...])
    fq = jnp.where(spot == 5, high, jnp.where(spot == 6, mid, jnp.where(spot == 7, low, fq_ref[0:slots, :])))
    fill(qa, jnp.where(low_half, q, fq), fq_ref, True, slots)
    fill(qb, jnp.where(low_half, fq, q), fq_ref, False, slots)
    k = k_ref[...]
    fill(ka, jnp.where(low_half, k, fk), fk_ref, True, slots)
    fill(kb, jnp.where(low_half, fk, k), fk_ref, False, slots)
    v = v_ref[...]
    one = jnp.ones_like(v)
    fill(va, jnp.where(low_half, v, one), None, True, slots)
    fill(vb, jnp.where(low_half, one, v), None, False, slots)
    g = g_ref[...]
    product = g.astype(F32) * wide_ref[...]
    delta_a = jnp.sum(jnp.where(low_half, product, 0.0), axis=1, keepdims=True)
    delta_b = jnp.sum(jnp.where(low_half, 0.0, product), axis=1, keepdims=True)
    high, mid, low = thirds(-jnp.where(low_half, delta_b, delta_a))
    zero = jnp.zeros_like(g)
    fg = jnp.where(spot == 0, high, jnp.where(spot == 1, mid, jnp.where(spot == 2, low, zero)))
    ga[...] = jnp.zeros_like(ga)
    gb[...] = jnp.zeros_like(gb)
    ga[0:slots, :] = jnp.where(low_half, g, fg)
    gb[0:slots, :] = jnp.where(low_half, fg, g)
    dqa[...] = jnp.zeros_like(dqa)
    dqb[...] = jnp.zeros_like(dqb)
    half = lax.broadcasted_iota(jnp.int32, (block, 128), 1) < HEAD_DIM

    def head(qx, kx, vx, gx, dqx, rows):
        keys = kx[rows, :]
        probs = jnp.exp(dot_nt(keys, qx[...]))
        value_grad = dot_nn(probs.astype(BF16), gx[...])
        score_grad = (probs * dot_nt(vx[rows, :], gx[...])).astype(BF16)
        key_grad = dot_nn(score_grad, qx[...])
        dqx[...] += dot_tn(score_grad, keys)
        return key_grad, value_grad

    def step(number, carry):
        rows = pl.ds(pl.multiple_of(number * block, 16), block)
        key_a, value_a = head(qa, ka, va, ga, dqa, rows)
        key_b, value_b = head(qb, kb, vb, gb, dqb, rows)
        dk[rows, :] = jnp.where(half, key_a, key_b)
        dv[rows, :] = jnp.where(half, value_a, value_b)
        return carry

    lax.fori_loop(0, dk.shape[0] // block, step, 0)
    dq_ref[...] = (jnp.where(low_half, dqa[0:slots, :], dqb[0:slots, :]) * 0.125).astype(BF16)
    dk_ref[...] = dk[0:slots, :].astype(BF16)
    dv_ref[...] = dv[0:slots, :].astype(BF16)


def attention_backward(qkv, upstream, wide_out, lse, fq, fk, block=240):
    slots = qkv.shape[0]
    pairs = qkv.shape[1] // 384
    wide = fq.shape[0]
    rows = round_up(slots, block)
    whole = pl.BlockSpec((wide, 128), lambda p: (0, 0))
    width = pairs * 128
    return pl.pallas_call(
        partial(backward_kernel, slots, block),
        grid=(pairs,),
        in_specs=[column(0, slots), column(pairs, slots), column(2 * pairs, slots),
                  column(0, slots), column(0, slots), column(0, slots), whole, whole],
        out_specs=[column(0, slots)] * 3,
        out_shape=[jax.ShapeDtypeStruct((slots, width), BF16)] * 3,
        scratch_shapes=[pltpu.VMEM((wide, 128), BF16)] * 8
        + [pltpu.VMEM((wide, 128), F32)] * 2 + [pltpu.VMEM((rows, 128), F32)] * 2,
        compiler_params=pltpu.CompilerParams(vmem_limit_bytes=60 * 2 ** 20),
        name="attention_backward",
    )(qkv, qkv, qkv, upstream, wide_out, lse, fq, fk)


D = 768
FF = 3072


epsilon = 1e-06
root_half = 0.7071067811865476
inverse_root_tau = 0.3989422804014327


def normalize_keep(values, gain_vector, shift_vector):
    centred = values - jnp.mean(values, axis=-1, keepdims=True)
    inverse = lax.rsqrt(jnp.mean(centred * centred, axis=-1, keepdims=True) + epsilon)
    scaled = centred * inverse
    return (scaled * gain_vector + shift_vector, scaled, inverse)


def normalize_back(upstream, scaled, inverse, gain_vector):
    weighted = upstream * gain_vector
    centred = weighted - jnp.mean(weighted, axis=-1, keepdims=True)
    result = inverse * (centred - scaled * jnp.mean(weighted * scaled, axis=-1, keepdims=True))
    return (result, jnp.sum(upstream * scaled, axis=0), jnp.sum(upstream, axis=0))


def split_vectors(small_full):
    columns = small_full.astype(jnp.float32)
    pieces = [columns[:, number] for number in range(8)]
    return (pieces, columns[:, 8:].T.reshape(FF))


def per_device(
    tokens,
    cotangent,
    segments,
    padding,
    qkv_weight,
    qkv_moment,
    qkv_average,
    merge_weight,
    merge_moment,
    merge_average,
    expand_weight,
    expand_moment,
    expand_average,
    shrink_weight,
    shrink_moment,
    shrink_average,
    small_params,
    small_moment,
    small_average,
):
    masters = (qkv_weight, merge_weight, expand_weight, shrink_weight, small_params)
    lowered = tuple((master.astype(jnp.bfloat16) for master in masters))
    low_qkv, low_merge, low_expand, low_shrink, low_small = lowered
    axes = ("dp", "fsdp")
    own_rows = qkv_weight.shape[0]
    first = jnp.concatenate([low_qkv, low_small.reshape(own_rows, -1)], axis=1)
    first = lax.all_gather(first, axes, axis=0, tiled=True)
    second = jnp.concatenate([low_merge, low_expand], axis=1)
    second = lax.all_gather(second, axes, axis=0, tiled=True)
    shrink_full = lax.all_gather(low_shrink, axes, axis=0, tiled=True)
    qkv_full, small_full = first[:, : 3 * D], first[:, 3 * D :]
    merge_full, expand_full = second[:, :D], second[:, D:]
    pieces, bias_expand = split_vectors(small_full)
    gain_one, shift_one, bias_query, bias_value, bias_merge, gain_two, shift_two, bias_shrink = (
        pieces
    )
    inputs = tokens.astype(jnp.float32)
    query_mask, key_mask = mask_features(segments, padding, tokens.shape[0])
    norm_one, scaled_one, inverse_one = normalize_keep(inputs, gain_one, shift_one)
    norm_one_low = norm_one.astype(jnp.bfloat16)
    joined = jnp.dot(norm_one_low, qkv_full, preferred_element_type=jnp.float32)
    joined = joined + jnp.concatenate([bias_query, jnp.zeros((D,), jnp.float32), bias_value])
    joined_low = joined.astype(jnp.bfloat16)
    attended_low, attended_wide, logsums = attention_forward(joined_low, query_mask, key_mask)
    middle = (
        inputs + jnp.dot(attended_low, merge_full, preferred_element_type=jnp.float32) + bias_merge
    )
    norm_two, scaled_two, inverse_two = normalize_keep(middle, gain_two, shift_two)
    norm_two_low = norm_two.astype(jnp.bfloat16)
    before = jnp.dot(norm_two_low, expand_full, preferred_element_type=jnp.float32) + bias_expand
    after_low = jax.nn.gelu(before, approximate=False).astype(jnp.bfloat16)
    output = (
        middle + jnp.dot(after_low, shrink_full, preferred_element_type=jnp.float32) + bias_shrink
    )
    activations = output.astype(jnp.bfloat16)
    back_gain_one, back_gain_two = gain_one, gain_two
    outgoing = cotangent.astype(jnp.float32) * padding[:, None].astype(jnp.float32)
    outgoing_low = outgoing.astype(jnp.bfloat16)
    shrink_part = jnp.einsum(
        "sf,sd->fd", after_low, outgoing_low, preferred_element_type=jnp.float32
    )
    shrink_bias_part = jnp.sum(outgoing, axis=0)
    act_grad = jnp.einsum(
        "sd,fd->sf", outgoing_low, shrink_full, preferred_element_type=jnp.float32
    )
    cumulative = 0.5 * (1.0 + lax.erf(before * root_half))
    density = jnp.exp(-0.5 * before * before) * inverse_root_tau
    before_grad = (act_grad * (cumulative + before * density)).astype(jnp.bfloat16)
    expand_part = jnp.einsum(
        "sd,sf->df", norm_two_low, before_grad, preferred_element_type=jnp.float32
    )
    expand_bias_part = jnp.sum(before_grad.astype(jnp.float32), axis=0)
    up_two = jnp.einsum("sf,df->sd", before_grad, expand_full, preferred_element_type=jnp.float32)
    second_back, gain_two_part, shift_two_part = normalize_back(
        up_two, scaled_two, inverse_two, back_gain_two
    )
    middle_grad = outgoing + second_back
    middle_low = middle_grad.astype(jnp.bfloat16)
    merge_part = jnp.einsum(
        "sd,se->de", attended_low, middle_low, preferred_element_type=jnp.float32
    )
    merge_bias_part = jnp.sum(middle_low.astype(jnp.float32), axis=0)
    attended_grad = jnp.einsum(
        "se,de->sd", middle_low, merge_full, preferred_element_type=jnp.float32
    ).astype(jnp.bfloat16)
    query_grads, key_grads, value_grads = attention_backward(
        joined_low, attended_grad, attended_wide, logsums, query_mask, key_mask
    )
    qkv_grad_low = jnp.concatenate([query_grads, key_grads, value_grads], axis=1)
    qkv_part = jnp.einsum(
        "sd,sc->dc", norm_one_low, qkv_grad_low, preferred_element_type=jnp.float32
    )
    column_sums = jnp.sum(qkv_grad_low.astype(jnp.float32), axis=0)
    up_one = jnp.einsum("sc,dc->sd", qkv_grad_low, qkv_full, preferred_element_type=jnp.float32)
    first_back, gain_one_part, shift_one_part = normalize_back(
        up_one, scaled_one, inverse_one, back_gain_one
    )
    input_grad = middle_grad + first_back
    vector_rows = jnp.stack(
        [
            gain_one_part,
            shift_one_part,
            column_sums[:D],
            column_sums[2 * D :],
            merge_bias_part,
            gain_two_part,
            shift_two_part,
            shrink_bias_part,
        ]
    )
    all_rows = jnp.concatenate([vector_rows, expand_bias_part.reshape(FF // D, D)], axis=0)
    small_part = all_rows.T
    wide_part = jnp.concatenate([merge_part, expand_part], axis=1).astype(BF16)
    last_part = jnp.concatenate([qkv_part, small_part], axis=1).astype(BF16)
    shrink_sum = lax.psum_scatter(shrink_part.astype(BF16), axes, scatter_dimension=0, tiled=True)
    wide_sum = lax.psum_scatter(wide_part, axes, scatter_dimension=0, tiled=True).astype(F32)
    last_sum = lax.psum_scatter(last_part, axes, scatter_dimension=0, tiled=True).astype(F32)
    summed = (
        last_sum[:, : 3 * D],
        wide_sum[:, :D],
        wide_sum[:, D:],
        shrink_sum.astype(F32),
        last_sum[:, 3 * D :].reshape(-1),
    )
    rate_scale = (tokens.shape[0] * lax.axis_size("dp") * lax.axis_size("fsdp")) ** (-0.5)
    rates = (
        0.04 * rate_scale,
        4.0 * rate_scale,
        0.08 * rate_scale,
        0.02 * rate_scale,
        0.07 * rate_scale,
    )
    moments = (qkv_moment, merge_moment, expand_moment, shrink_moment, small_moment)
    averages = (qkv_average, merge_average, expand_average, shrink_average, small_average)
    results = [activations, input_grad]
    for master, gradient, moment, average, step_rate in zip(
        masters, summed, moments, averages, rates
    ):
        fresh_moment = 0.5 * moment + gradient
        updated = master - step_rate * (gradient + 0.5 * fresh_moment)
        results.extend(
            [
                gradient,
                fresh_moment,
                updated,
                0.5 * average + 0.5 * updated,
                updated.astype(jnp.bfloat16),
            ]
        )
    return tuple(results)


def solution(mesh):
    placed = (
        P(("dp", "fsdp"), None),
        P(("dp", "fsdp"), None),
        P(("dp", "fsdp")),
        P(("dp", "fsdp")),
        P(("dp", "fsdp"), None),
        P(("dp", "fsdp"), None),
        P(("dp", "fsdp"), None),
        P(("dp", "fsdp"), None),
        P(("dp", "fsdp"), None),
        P(("dp", "fsdp"), None),
        P(("dp", "fsdp"), None),
        P(("dp", "fsdp"), None),
        P(("dp", "fsdp"), None),
        P(("dp", "fsdp"), None),
        P(("dp", "fsdp"), None),
        P(("dp", "fsdp"), None),
        P(("dp", "fsdp")),
        P(("dp", "fsdp")),
        P(("dp", "fsdp")),
    )
    return jax.shard_map(
        per_device,
        mesh=mesh,
        in_specs=placed,
        out_specs=(
            P(("dp", "fsdp"), None),
            P(("dp", "fsdp"), None),
            P(("dp", "fsdp"), None),
            P(("dp", "fsdp"), None),
            P(("dp", "fsdp"), None),
            P(("dp", "fsdp"), None),
            P(("dp", "fsdp"), None),
            P(("dp", "fsdp"), None),
            P(("dp", "fsdp"), None),
            P(("dp", "fsdp"), None),
            P(("dp", "fsdp"), None),
            P(("dp", "fsdp"), None),
            P(("dp", "fsdp"), None),
            P(("dp", "fsdp"), None),
            P(("dp", "fsdp"), None),
            P(("dp", "fsdp"), None),
            P(("dp", "fsdp"), None),
            P(("dp", "fsdp"), None),
            P(("dp", "fsdp"), None),
            P(("dp", "fsdp"), None),
            P(("dp", "fsdp"), None),
            P(("dp", "fsdp"), None),
            P(("dp", "fsdp")),
            P(("dp", "fsdp")),
            P(("dp", "fsdp")),
            P(("dp", "fsdp")),
            P(("dp", "fsdp")),
        ),
        check_vma=False,
    )
```

time: 1750 us -> 761 us (0.43)
  other arithmetic: 630 us -> 39.4 us
  local copies, waits for them, and re-layouts: 272 us -> 26 us
  matrix products: 330 us -> 141 us
  Pallas kernels: 0 us -> 121 us
  blocking collectives: 82.5 us -> 0 us
    sub x6 -> x0, other arithmetic: 424 us -> none  [pair_backward(): score_grad = (probs * (prob_grad - row_terms)).astype(jnp.bfloat16)]
    dot_general x12 -> x0, local copies, waits for them, and re-layouts: 237 us -> none  [the longest x6 119 us: pair_backward(): jnp.einsum('qhd,khd->hqk', upstream_pair, value_pair, preferred_element_t...]
    dot_general x46 -> x4, matrix products: 229 us -> 40.1 us  [the longest x1 14.4 us: per_device(): jnp.einsum('sd,fd->sf', outgoing_low, shrink_full, preferred_element_type...]
    convert_element_type x6 -> x2, other arithmetic: 142 us -> 1.26 us  [the longest x1 0.95 us: split_vectors(): columns = small_full.astype(jnp.float32)]
    pallas_call x0 -> x2, Pallas kernels: none -> 121 us  [the longest x1 75.8 us: attention_backward(): pl.pallas_call(partial(backward_kernel, slots, block), grid=(pairs,), in_...]
    unnamed x2 -> x0, blocking collectives: 82.5 us -> none
    reduce_scatter x4 -> x2, waiting for transfers between devices: 301 us -> 220 us  [the longest x1 113 us: per_device(): lax.psum_scatter(wide_part, axes, scatter_dimension=0, tiled=True)]
    unnamed x8 -> x7, waiting for transfers between devices: 0.13 us -> 55.8 us
  transfers between devices with their start and end apart: 8 -> 6, of which waited for: 6 -> 6; matrix products, arithmetic and copies ran while one was open for 65% -> 8% of each run, Pallas kernels for 0% -> 6%
where the time goes in v1:
time: 761 us; the launch traced here: 753 us
  waiting for transfers between devices  410 us (54%)
  matrix products  141 us (19%)
  Pallas kernels  121 us (16%)
  other arithmetic  39.4 us (5%)
  local copies, waits for them, and re-layouts  26 us (3%)
  between operations  15.4 us (2%)
    reduce_scatter x1, waiting for transfers between devices, per_device(): lax.psum_scatter(wide_part, axes, scatter_dimension=0, tiled=True)  113 us
    reduce_scatter x1, waiting for transfers between devices, per_device(): lax.psum_scatter(shrink_part.astype(BF16), axes, scatter_dimension=0, til...  106 us
    pallas_call x1, Pallas kernels, attention_backward(): pl.pallas_call(partial(backward_kernel, slots, block), grid=(pairs,), in_...  75.8 us
    all_gather x1, waiting for transfers between devices, per_device(): shrink_full = lax.all_gather(low_shrink, axes, axis=0, tiled=True)  62.8 us
    all_gather x1, waiting for transfers between devices, per_device(): first = lax.all_gather(first, axes, axis=0, tiled=True)  58.7 us
    unnamed x7, waiting for transfers between devices  55.8 us
    dot_general x1, matrix products, per_device(): jnp.dot(norm_two_low, expand_full, preferred_element_type=jnp.float32)  48.6 us
    pallas_call x1, Pallas kernels, attention_forward(): pl.pallas_call(partial(forward_kernel, slots, block), grid=(pairs,), in_s...  45.1 us
  transfers between devices with their start and end apart: 6, of which 6 were waited for; matrix products, arithmetic and copies ran while one was open for 8% of the time, Pallas kernels for 6%

profile of v1, /device:TPU:0, one launch (start us, length us, event | category | flops | bytes accessed | tf_op | source)
XLA Modules:
  0.0 752.6 jit_solution(8671576265509116413)
XLA Ops:
  7.3 0.8 convert_element_type.101
  8.2 1.0 convert_element_type.100
  9.1 0.7 pad_maximum_fusion.3
  9.9 1.0 convert_element_type.108
  10.8 0.9 convert_element_type.107
  11.7 0.7 pad_maximum_fusion.2
  12.5 0.8 fusion.60
  13.3 1.8 convert_reduce_fusion
  15.2 0.7 fusion.36
  16.2 58.7 %all-gather.4.cloned.1.call-done = bf16[768,2316]{1,0:T(8,128)(2,1)} async-done(((bf16[24,2316]{1,0:T(8,128)(2,1)}), bf16[768,2316]{1,0:T(8,128)(2,1)}) %all-gather.4.cloned.1.call-update) | async-done | bytes 3557392 | tf_op jit(solution)/shard_map/all_gather | solution.py:256
  74.8 1.0 slice_convert_fusion
  76.1 1.6 slice_reduce_fusion
  77.8 8.7 %fusion.16.q_ref.k_ref.v_ref = bf16[1190,2304]{1,0:T(8,128)(2,1)} fusion(f32[2304]{0:T(1024)S(1)} %pad_maximum_fusion.4, bf16[768,2316]{1,0:T(8,128)(2,1)} %all-gather.4.cloned.1.call-done, bf16[1190,768]{1,0:T(8,128)(2,1)S(1)} %copy-done.4, f32[768]{0:T(1024)S(1)} %get-tuple-element.53, f32[768]{0:T(1024)S(1)} %get-tuple-element.54, ...), kind=kOutput, calls=%fused_computation.27 | convolution fusion | flops 4222310400 | bytes 10875184 | tf_op jit(solution)/shard_map/dot_general | solution.py:270
  86.6 45.1 %attention_forward.1 = (bf16[1190,768]{1,0:T(8,128)(2,1)S(1)}, f32[1190,768]{1,0:T(8,128)}, f32[1190,768]{1,0:T(8,128)}) custom-call(bf16[1190,2304]{1,0:T(8,128)(2,1)} %fusion.16.q_ref.k_ref.v_ref, bf16[1190,2304]{1,0:T(8,128)(2,1)} %fusion.16.q_ref.k_ref.v_ref, bf16[1190,2304]{1,0:T(8,128)(2,1)} %fusion.16.q_ref.k_ref.v_ref, ...), custom_call_target="tpu_custom_call" | custom-call | tf_op jit(solution)/shard_map/attention_forward/pallas_call | solution.py:100
  131.6 13.0 %all-gather.6.cloned.1.call-done = bf16[768,3840]{1,0:T(8,128)(2,1)} async-done(((bf16[24,3840]{1,0:T(8,128)(2,1)}), bf16[768,3840]{1,0:T(8,128)(2,1)}) %all-gather.6.cloned.1.call-update) | async-done | bytes 5898256 | tf_op jit(solution)/shard_map/all_gather | solution.py:258
  144.7 3.8 fusion.62
  149.2 48.6 %fusion.2 = (bf16[1190,3072]{1,0:T(8,128)(2,1)S(1)}, f32[1190,3072]{1,0:T(8,128)}) fusion(f32[3072]{0:T(1024)S(1)} %add.180, bf16[768,3840]{1,0:T(8,128)(2,1)S(1)} %bitcast.15, f32[1190,768]{1,0:T(8,128)S(1)} %get-tuple-element.84, f32[768]{0:T(1024)S(1)} %get-tuple-element.48, f32[768]{0:T(1024)S(1)} %get-tuple-element.49, f32[1190]{0:T(1024)S(1)} %add_rsqrt_fusion, ...), kind=kOutput, calls=%fused_computation.4 | convolution fusion | flops 5860968960 | bytes 30351360 | tf_op jit(solution)/shard_map/dot_general | solution.py:279
  197.8 2.9 copy-done.57
  200.7 8.8 %convolution_convert_fusion.1 = bf16[3072,768]{1,0:T(8,128)(2,1)} fusion(bf16[1190,3072]{1,0:T(8,128)(2,1)S(1)} %get-tuple-element.85, bf16[1190,768]{1,0:T(8,128)(2,1)S(1)} %copy-done.12, f32[1190]{0:T(1024)S(1)} %get-tuple-element.79), kind=kOutput, calls=%fused_computation.33 | convolution fusion | flops 5620225536 | bytes 13862552 | tf_op jit(solution)/shard_map/sf,sd->fd/dot_general | solution.py:288
  209.5 106.3 %reduce-scatter.8.cloned.1.call-done = bf16[96,768]{1,0:T(8,128)(2,1)} async-done(((bf16[3072,768]{1,0:T(8,128)(2,1)}), bf16[96,768]{1,0:T(8,128)(2,1)}) %reduce-scatter.8.cloned.1.call-update) | async-done | bytes 147472 | tf_op jit(solution)/shard_map/reduce_scatter | solution.py:344
  315.8 2.0 fusion.56
  318.3 0.6 stack.39
  318.9 62.8 %all-gather.8.cloned.1.call-done = bf16[3072,768]{1,0:T(8,128)(2,1)} async-done(((bf16[96,768]{1,0:T(8,128)(2,1)}), bf16[3072,768]{1,0:T(8,128)(2,1)}) %all-gather.8.cloned.1.call-update) | async-done | bytes 4718608 | tf_op jit(solution)/shard_map/all_gather | solution.py:259
  381.7 14.4 %fusion.63 = (bf16[3072]{0:T(1024)(128)(2,1)}, bf16[1190,3072]{1,0:T(8,128)(2,1)S(1)}) fusion(f32[1190,3072]{1,0:T(8,128)} %get-tuple-element.86, f32[3072]{0:T(1024)S(1)} %add.180, bf16[3072,768]{1,0:T(8,128)(2,1)} %all-gather.8.cloned.1.call-done, bf16[1190,768]{1,0:T(8,128)(2,1)S(1)} %copy-done.12, f32[1190]{0:T(1024)S(1)} %get-tuple-element.79), kind=kOutput, calls=%fused_computation.140 | convolution fusion | flops 5661731328 | bytes 28503704 | tf_op jit(solution)/shard_map/sd,fd->sf/dot_general | solution.py:292
  396.1 12.8 %multiply_reduce_fusion = (bf16[768]{0:T(1024)(128)(2,1)}, f32[1190]{0:T(1024)S(1)}, f32[1190]{0:T(1024)S(1)}, bf16[768]{0:T(1024)(128)(2,1)}, f32[1190,768]{1,0:T(8,128)S(1)}) fusion(f32[1190,768]{1,0:T(8,128)S(1)} %copy-done.8, f32[1190]{0:T(1024)S(1)} %add_rsqrt_fusion, f32[1190]{0:T(1024)S(1)} %broadcast_multiply_fusion.4, ...), kind=kOutput, calls=%fused_computation.57 | convolution fusion | flops 5623346176 | bytes 19366496 | tf_op jit(solution)/shard_map/sf,df->sd/dot_general | solution.py:302
  408.9 2.4 convert_reduce_fusion.1
  411.3 5.1 convolution_convert_fusion.3.g_ref
  416.4 75.8 %attention_backward.1 = (bf16[1190,768]{1,0:T(8,128)(2,1)}, bf16[1190,768]{1,0:T(8,128)(2,1)}, bf16[1190,768]{1,0:T(8,128)(2,1)}) custom-call(bf16[1190,2304]{1,0:T(8,128)(2,1)} %fusion.16.q_ref.k_ref.v_ref, bf16[1190,2304]{1,0:T(8,128)(2,1)} %fusion.16.q_ref.k_ref.v_ref, bf16[1190,2304]{1,0:T(8,128)(2,1)} %fusion.16.q_ref.k_ref.v_ref, ...), custom_call_target="tpu_custom_call" | custom-call | tf_op jit(solution)/shard_map/attention_backward/pallas_call | solution.py:186
  492.2 1.8 constant_dynamic-update-slice_fusion.2
  494.9 1.0 copy-done.5
  495.9 5.7 convolution_convert_fusion
  501.6 7.8 %fusion.35 = (bf16[768]{0:T(1024)(128)(2,1)S(1)}, f32[1190]{0:T(1024)}, f32[1190]{0:T(1024)}, bf16[768]{0:T(1024)(128)(2,1)S(1)}, f32[1190,768]{1,0:T(8,128)}) fusion(bf16[1190,768]{1,0:T(8,128)(2,1)S(1)} %copy-done.5, f32[1190]{0:T(1024)S(1)} %copy-done.34, f32[1190]{0:T(1024)S(1)} %copy-done.32, f32[768]{0:T(1024)S(1)} %copy-done.39, ...), kind=kOutput, calls=%fused_computation.55 | convolution fusion | flops 4220478464 | bytes 14551344 | tf_op jit(solution)/shard_map/sc,dc->sd/dot_general | solution.py:323
  509.4 0.6 stack.32
  510.0 0.6 stack.33
  510.6 4.0 reduce
  514.5 0.7 fusion.61
  515.2 0.6 stack.34
  516.4 1.3 stack.36
  517.7 1.3 stack.37
  518.9 1.3 stack.38
  520.2 1.3 reshape.116
  521.5 2.7 concatenate.32
  524.2 1.6 copy.59
  525.8 3.1 pad_maximum_fusion.1
  529.0 1.4 copy-done.3
  530.4 3.8 convolution_convert_fusion.4
  534.2 0.9 copy.60
  535.2 10.8 %convolution_convert_fusion.2 = bf16[768,3072]{1,0:T(8,128)(2,1)S(1)} fusion(bf16[1190,3072]{1,0:T(8,128)(2,1)} %copy-done.56, f32[1190,768]{1,0:T(8,128)} %copy-done.7, f32[768]{0:T(1024)S(1)} %copy-done.51, f32[768]{0:T(1024)S(1)} %copy-done.42, f32[1190]{0:T(1024)S(1)} %copy-done.37, f32[1190]{0:T(1024)S(1)} %broadcast_multiply_fusion.4), kind=kOutput, calls=%fused_computation.34 | convolution fusion | flops 5622053376 | bytes 15701296 | tf_op jit(solution)/shard_map/sd,sf->df/dot_general | solution.py:298
  546.0 2.9 pad_maximum_fusion
  549.0 0.9 copy-done.15
  550.0 0.7 add_multiply_fusion
  550.8 5.4 fusion.34
  556.3 10.7 %fusion.39 = bf16[1190,768]{1,0:T(8,128)(2,1)} fusion(f32[1190,768]{1,0:T(8,128)S(1)} %copy-done.9, bf16[1190,3072]{1,0:T(8,128)(2,1)} %copy-done.57, bf16[3072,768]{1,0:T(8,128)(2,1)} %all-gather.8.cloned.1.call-done, f32[768]{0:T(1024)S(1)} %copy-done.49), kind=kOutput, calls=%fused_computation.66 | convolution fusion | flops 5617866240 | bytes 17516544 | tf_op jit(solution)/shard_map/dot_general | solution.py:282
  567.0 55.7 %reduce-scatter.10.cloned.1.call-done = bf16[24,2316]{1,0:T(8,128)(2,1)} async-done(((bf16[768,2316]{1,0:T(8,128)(2,1)}), bf16[24,2316]{1,0:T(8,128)(2,1)}) %reduce-scatter.10.cloned.1.call-update) | async-done | bytes 111184
  622.7 0.7 slice.96
  623.5 0.6 fusion.55
  624.1 0.6 add_multiply_fusion.4
  624.7 1.7 fusion.59
  626.4 0.8 add_multiply_fusion.2
  627.2 113.3 %reduce-scatter.6.cloned.1.call-done = bf16[24,3840]{1,0:T(8,128)(2,1)} async-done(((bf16[768,3840]{1,0:T(8,128)(2,1)}), bf16[24,3840]{1,0:T(8,128)(2,1)}) %reduce-scatter.6.cloned.1.call-update) | async-done | bytes 184336 | tf_op jit(solution)/shard_map/reduce_scatter | solution.py:345
  740.5 1.4 fusion.58
  742.0 0.7 add_multiply_fusion.3
  742.6 1.8 fusion.57
  744.5 0.8 add_multiply_fusion.1
  (153 shorter events, 4.1 us)
Async XLA Ops:
  7.2 7.9 %copy-start.4 = (bf16[1190,768]{1,0:T(8,128)(2,1)S(1)}, bf16[1190,768]{1,0:T(8,128)(2,1)}, u32[]{:S(2)}) copy-start(bf16[1190,768]{1,0:T(8,128)(2,1)} %param.19) | copy-start | bytes 5483524
  7.2 67.6 %all-gather.4.cloned.1.call-start = ((), (), s32[]{:S(2)}) async-start(), calls=%async_computation.3 | async-start | bytes 3852288 | tf_op jit(solution)/shard_map/all_gather | solution.py:256
  9.8 134.9 %all-gather.6.cloned.1.call-start = ((), (), s32[]{:S(2)}) async-start(), calls=%async_computation.4 | async-start | bytes 6082560 | tf_op jit(solution)/shard_map/all_gather | solution.py:258
  12.4 303.4 %reduce-scatter.8.cloned.1.call-start = ((), (), s32[]{:S(2)}) async-start(), calls=%async_computation.7 | async-start | bytes 4866048 | tf_op jit(solution)/shard_map/reduce_scatter | solution.py:344
  15.1 62.7 %copy-start.31 = (f32[1190]{0:T(1024)}, f32[1190]{0:T(1024)S(1)}, u32[]{:S(2)}) copy-start(f32[1190]{0:T(1024)S(1)} %broadcast_multiply_fusion.5) | copy-start | bytes 14284
  15.9 70.7 %copy-start.33 = (f32[1190]{0:T(1024)}, f32[1190]{0:T(1024)S(1)}, u32[]{:S(2)}) copy-start(f32[1190]{0:T(1024)S(1)} %add_rsqrt_fusion.1) | copy-start | bytes 14284
  16.2 70.4 %copy-start = (bf16[1280,128]{1,0:T(8,128)(2,1)}, bf16[1280,128]{1,0:T(8,128)(2,1)S(1)}, u32[]{:S(2)}) copy-start(bf16[1280,128]{1,0:T(8,128)(2,1)S(1)} %get-tuple-element.77.fk_ref) | copy-start | bytes 983044
  16.2 70.4 %copy-start.1 = (bf16[1280,128]{1,0:T(8,128)(2,1)}, bf16[1280,128]{1,0:T(8,128)(2,1)S(1)}, u32[]{:S(2)}) copy-start(bf16[1280,128]{1,0:T(8,128)(2,1)S(1)} %get-tuple-element.78.fq_ref) | copy-start | bytes 983044
  77.8 8.8 %copy-start.38 = (f32[768]{0:T(1024)}, f32[768]{0:T(1024)S(1)}, u32[]{:S(2)}) copy-start(f32[768]{0:T(1024)S(1)} %get-tuple-element.54) | copy-start | bytes 9220
  77.8 8.8 %copy-start.52 = (f32[768]{0:T(1024)}, f32[768]{0:T(1024)S(1)}, u32[]{:S(2)}) copy-start(f32[768]{0:T(1024)S(1)} %get-tuple-element.53) | copy-start | bytes 9220
  77.8 71.3 %copy-start.50 = (f32[768]{0:T(1024)}, f32[768]{0:T(1024)S(1)}, u32[]{:S(2)}) copy-start(f32[768]{0:T(1024)S(1)} %get-tuple-element.48) | copy-start | bytes 9220
  77.8 331.1 %copy-start.41 = (f32[768]{0:T(1024)}, f32[768]{0:T(1024)S(1)}, u32[]{:S(2)}) copy-start(f32[768]{0:T(1024)S(1)} %get-tuple-element.49) | copy-start | bytes 9220
  131.6 16.9 %copy-start.2 = (bf16[1190,768]{1,0:T(8,128)(2,1)}, bf16[1190,768]{1,0:T(8,128)(2,1)S(1)}, u32[]{:S(2)}) copy-start(bf16[1190,768]{1,0:T(8,128)(2,1)S(1)} %get-tuple-element.33) | copy-start | bytes 5483524
  144.7 4.5 slice-start
  144.7 4.5 slice-start.1
  148.5 49.2 %copy-start.7 = (f32[1190,768]{1,0:T(8,128)}, f32[1190,768]{1,0:T(8,128)S(1)}, u32[]{:S(2)}) copy-start(f32[1190,768]{1,0:T(8,128)S(1)} %get-tuple-element.84) | copy-start | bytes 10967044
  149.1 259.8 %copy-start.36 = (f32[1190]{0:T(1024)}, f32[1190]{0:T(1024)S(1)}, u32[]{:S(2)}) copy-start(f32[1190]{0:T(1024)S(1)} %add_rsqrt_fusion) | copy-start | bytes 14284
  149.2 51.5 %copy-start.12 = (bf16[1190,768]{1,0:T(8,128)(2,1)S(1)}, bf16[1190,768]{1,0:T(8,128)(2,1)}, u32[]{:S(2)}) copy-start(bf16[1190,768]{1,0:T(8,128)(2,1)} %param.20) | copy-start | bytes 5483524
  197.8 2.9 copy-start.57
  209.5 106.4 %copy-start.24 = (f32[96,768]{1,0:T(8,128)S(1)}, f32[96,768]{1,0:T(8,128)}, u32[]{:S(2)}) copy-start(f32[96,768]{1,0:T(8,128)} %param.32) | copy-start | bytes 884740
  209.5 106.4 %copy-start.25 = (f32[96,768]{1,0:T(8,128)S(1)}, f32[96,768]{1,0:T(8,128)}, u32[]{:S(2)}) copy-start(f32[96,768]{1,0:T(8,128)} %param.33) | copy-start | bytes 884740
  209.5 172.2 %all-gather.8.cloned.1.call-start = ((), (), s32[]{:S(2)}) async-start(), calls=%async_computation.5 | async-start | bytes 4866048 | tf_op jit(solution)/shard_map/all_gather | solution.py:259
  317.8 304.9 %reduce-scatter.10.cloned.1.call-start = ((), (), s32[]{:S(2)}) async-start(), calls=%async_computation.8 | async-start | bytes 3852288
  381.7 14.4 %copy-start.8 = (f32[1190,768]{1,0:T(8,128)S(1)}, f32[1190,768]{1,0:T(8,128)}, u32[]{:S(2)}) copy-start(f32[1190,768]{1,0:T(8,128)} %copy-done.7) | copy-start | bytes 10967044
  396.1 12.8 %copy-start.56 = (bf16[1190,3072]{1,0:T(8,128)(2,1)}, bf16[1190,3072]{1,0:T(8,128)(2,1)S(1)}, u32[]{:S(2)}) copy-start(bf16[1190,3072]{1,0:T(8,128)(2,1)S(1)} %get-tuple-element.90) | copy-start | bytes 21934084
  411.3 5.1 copy-start.10
  492.1 2.0 copy-start.14
  492.2 2.6 copy-start.13
  494.2 1.6 copy-start.5
  494.2 1.6 copy-start.32
  494.2 1.6 copy-start.34
  494.2 1.6 copy-start.39
  494.2 1.6 copy-start.53
  495.8 5.7 copy-start.11
  495.9 5.7 copy-start.43
  528.9 1.5 copy-start.3
  528.9 6.2 copy-start.37
  529.0 6.2 copy-start.42
  529.0 6.2 copy-start.51
  529.0 211.5 %reduce-scatter.6.cloned.1.call-start = ((), (), s32[]{:S(2)}) async-start(), calls=%async_computation.6 | async-start | bytes 6082560 | tf_op jit(solution)/shard_map/reduce_scatter | solution.py:345
  548.9 1.1 copy-start.20
  548.9 1.8 copy-start.45
  548.9 1.8 copy-start.44
  548.9 1.8 copy-start.6
  548.9 1.8 copy-start.35
  548.9 1.8 copy-start.40
  550.8 5.4 copy-start.9
  550.8 5.4 copy-start.49
  556.2 67.3 %copy-start.48 = (f32[288]{0:T(512)S(1)}, f32[288]{0:T(512)}, u32[]{:S(2)}) copy-start(f32[288]{0:T(512)} %param.35) | copy-start | bytes 3460
  556.2 67.3 %copy-start.55 = (f32[288]{0:T(512)S(1)}, f32[288]{0:T(512)}, u32[]{:S(2)}) copy-start(f32[288]{0:T(512)} %param.36) | copy-start | bytes 3460
  556.2 67.9 %copy-start.54 = (f32[288]{0:T(512)S(1)}, f32[288]{0:T(512)}, u32[]{:S(2)}) copy-start(f32[288]{0:T(512)} %param.37) | copy-start | bytes 3460
  556.2 68.5 %copy-start.18 = (f32[24,2304]{1,0:T(8,128)S(1)}, f32[24,2304]{1,0:T(8,128)}, u32[]{:S(2)}) copy-start(f32[24,2304]{1,0:T(8,128)} %param.23) | copy-start | bytes 663556
  556.2 68.5 %copy-start.28 = (f32[24,2304]{1,0:T(8,128)S(1)}, f32[24,2304]{1,0:T(8,128)}, u32[]{:S(2)}) copy-start(f32[24,2304]{1,0:T(8,128)} %param.24) | copy-start | bytes 663556
  556.2 70.2 %copy-start.27 = (f32[24,2304]{1,0:T(8,128)S(1)}, f32[24,2304]{1,0:T(8,128)}, u32[]{:S(2)}) copy-start(f32[24,2304]{1,0:T(8,128)} %param.25) | copy-start | bytes 663556
  556.2 184.3 %copy-start.23 = (f32[24,768]{1,0:T(8,128)S(1)}, f32[24,768]{1,0:T(8,128)}, u32[]{:S(2)}) copy-start(f32[24,768]{1,0:T(8,128)} %param.26) | copy-start | bytes 221188
  556.2 184.3 %copy-start.30 = (f32[24,768]{1,0:T(8,128)S(1)}, f32[24,768]{1,0:T(8,128)}, u32[]{:S(2)}) copy-start(f32[24,768]{1,0:T(8,128)} %param.27) | copy-start | bytes 221188
  556.2 185.7 %copy-start.29 = (f32[24,768]{1,0:T(8,128)S(1)}, f32[24,768]{1,0:T(8,128)}, u32[]{:S(2)}) copy-start(f32[24,768]{1,0:T(8,128)} %param.28) | copy-start | bytes 221188
  556.3 186.4 %copy-start.17 = (f32[24,3072]{1,0:T(8,128)S(1)}, f32[24,3072]{1,0:T(8,128)}, u32[]{:S(2)}) copy-start(f32[24,3072]{1,0:T(8,128)} %param.29) | copy-start | bytes 884740
  556.3 186.3 %copy-start.26 = (f32[24,3072]{1,0:T(8,128)S(1)}, f32[24,3072]{1,0:T(8,128)}, u32[]{:S(2)}) copy-start(f32[24,3072]{1,0:T(8,128)} %param.30) | copy-start | bytes 884740
  567.0 177.5 %copy-start.21 = (f32[24,3072]{1,0:T(8,128)S(1)}, f32[24,3072]{1,0:T(8,128)}, u32[]{:S(2)}) copy-start(f32[24,3072]{1,0:T(8,128)} %param.31) | copy-start | bytes 884740
  623.5 121.7 %copy-start.46 = (f32[288]{0:T(512)}, f32[288]{0:T(512)S(1)}, u32[]{:S(2)}) copy-start(f32[288]{0:T(512)S(1)} %reshape.117) | copy-start | bytes 3460
  624.1 121.1 %copy-start.47 = (f32[288]{0:T(512)}, f32[288]{0:T(512)S(1)}, u32[]{:S(2)}) copy-start(f32[288]{0:T(512)S(1)} %get-tuple-element.56) | copy-start | bytes 3460
  626.4 118.8 %copy-start.19 = (f32[24,2304]{1,0:T(8,128)}, f32[24,2304]{1,0:T(8,128)S(1)}, u32[]{:S(2)}) copy-start(f32[24,2304]{1,0:T(8,128)S(1)} %get-tuple-element.71) | copy-start | bytes 663556
  742.0 3.3 copy-start.22
  (2 other events, 1.8 us)
Sparse Core Ops, SparseCore 0:
  11.4 63.3 all-gather.3
  78.3 66.3 all-gather.5
  209.6 106.1 reduce-scatter.7
  319.1 62.4 all-gather.7
  529.1 93.5 reduce-scatter.9
  628.2 112.2 reduce-scatter.5

commit v2 on v1

--- a/solution.py
+++ b/solution.py
@@ -197,6 +197,238 @@
     )(qkv, qkv, qkv, upstream, wide_out, lse, fq, fk)
 
 
+MESH = pl.DeviceIdType.MESH
+
+
+class Place:
+    def __init__(self, n_dp, n_fsdp):
+        self.n_dp, self.n_fsdp, self.lines = n_dp, n_fsdp, n_fsdp // 4
+        self.dp, at = lax.axis_index("dp"), lax.axis_index("fsdp")
+        core = self.dp % 2
+        self.stride_u, self.stride_w = 2 - core, 1 + core
+        high, low = (at // 2) % 2, at % 2
+        self.a = at // 4
+        self.u = high * (1 - core) + low * core
+        self.w = low * (1 - core) + high * core
+
+    def fsdp_of(self, da, du, dw):
+        a, u, w = (self.a + da) % self.lines, (self.u + du) % 2, (self.w + dw) % 2
+        return a * 4 + u * self.stride_u + w * self.stride_w
+
+    def dp_of(self, dd):
+        return (self.dp + dd) % self.n_dp
+
+    def piece(self, dd, da, du, dw):
+        return self.dp_of(dd) * self.n_fsdp + self.fsdp_of(da, du, dw)
+
+    def device(self, dd, da, du, dw):
+        return (self.dp_of(dd), self.fsdp_of(da, du, dw))
+
+    def slot(self, dd, da, du, dw):
+        return ((dd * self.lines + da) * 2 + du) * 2 + dw
+
+    def greet(self):
+        barrier = pltpu.get_barrier_semaphore()
+        friends = [(0, 0, 1, 0), (0, 0, 0, 1)]
+        friends += [(0, da, 0, 0) for da in range(1, self.lines)]
+        friends += [(dd, 0, 0, 0) for dd in range(1, self.n_dp)]
+        for friend in friends:
+            pl.semaphore_signal(barrier, inc=1, device_id=self.device(*friend), device_id_type=MESH)
+        pl.semaphore_wait(barrier, len(friends))
+
+
+class Sender:
+    def __init__(self, place, send_sem):
+        self.place, self.send_sem, self.pending = place, send_sem, []
+
+    def send(self, source, target, recv_sem, device):
+        copy = pltpu.make_async_remote_copy(
+            src_ref=source, dst_ref=target, send_sem=self.send_sem.at[len(self.pending)],
+            recv_sem=recv_sem, device_id=self.place.device(*device), device_id_type=MESH,
+        )
+        copy.start()
+        self.pending.append(copy)
+
+    def arrived(self, target, recv_sem):
+        pltpu.make_async_remote_copy(
+            src_ref=target, dst_ref=target, send_sem=self.send_sem.at[0],
+            recv_sem=recv_sem, device_id=self.place.device(0, 0, 0, 1), device_id_type=MESH,
+        ).wait_recv()
+
+    def drain(self):
+        for copy in self.pending:
+            copy.wait_send()
+
+
+def gather_kernel(n_dp, n_fsdp, count, *refs):
+    own, full = refs[:count], refs[count : 2 * count]
+    send_sem, recv_sem, local_sem = refs[2 * count :]
+    place = Place(n_dp, n_fsdp)
+    sender = Sender(place, send_sem)
+    lines = place.lines
+    here = [pltpu.make_async_copy(own[i], full[i].at[place.piece(0, 0, 0, 0)], local_sem.at[i]) for i in range(count)]
+    for copy in here:
+        copy.start()
+    place.greet()
+
+    def forward(piece, device, source=None):
+        dd, da, du, dw = piece
+        ed, ea, eu, ew = device
+        bits = ((du - eu) % 2, (dw - ew) % 2)
+        seen = place.slot((dd - ed) % n_dp, (da - ea) % lines, *(bits[::-1] if ed % 2 else bits))
+        for i in range(count):
+            target = full[i].at[place.piece(*piece)]
+            sender.send(target if source is None else source[i], target, recv_sem.at[seen * count + i], device)
+
+    def await_piece(piece):
+        for i in range(count):
+            sender.arrived(full[i].at[place.piece(*piece)], recv_sem.at[place.slot(*piece) * count + i])
+
+    spread_line = [(0, da, 0, 0) for da in range(1, lines)]
+    spread_dp = [(dd, 0, 0, 0) for dd in range(1, n_dp)]
+    last = [(0, 0, 0, 1)]
+    for device in [(0, 0, 1, 0)] + last + spread_line + spread_dp:
+        forward((0, 0, 0, 0), device, own)
+    await_piece((0, 0, 1, 0))
+    for device in last + spread_line + spread_dp:
+        forward((0, 0, 1, 0), device)
+    await_piece((0, 0, 0, 1))
+    for device in spread_dp:
+        forward((0, 0, 0, 1), device)
+    for da in sorted(range(1, lines), key=lambda d: min(d, lines - d)):
+        for du in range(2):
+            await_piece((0, da, du, 0))
+            for device in last + spread_dp:
+                forward((0, da, du, 0), device)
+    for da in range(lines):
+        for du in range(2):
+            if da or du:
+                await_piece((0, da, du, 1))
+                for device in spread_dp:
+                    forward((0, da, du, 1), device)
+    for dd in range(1, n_dp):
+        for da in range(lines):
+            for du in range(2):
+                for dw in range(2):
+                    await_piece((dd, da, du, dw))
+    for copy in here:
+        copy.wait()
+    sender.drain()
+
+
+def gather_pieces(pieces, n_dp, n_fsdp, collective_id):
+    count, lines, total = len(pieces), n_fsdp // 4, n_dp * n_fsdp
+    sends = (1 + 1 + (lines - 1) * 2 + 1 + (lines - 1) * 2 + n_fsdp * (n_dp - 1)) * count
+    return pl.pallas_call(
+        partial(gather_kernel, n_dp, n_fsdp, count),
+        in_specs=[pl.BlockSpec(memory_space=pltpu.VMEM)] * count,
+        out_specs=[pl.BlockSpec(memory_space=pltpu.VMEM)] * count,
+        out_shape=[jax.ShapeDtypeStruct((total,) + piece.shape, piece.dtype) for piece in pieces],
+        scratch_shapes=[
+            pltpu.SemaphoreType.DMA((sends,)),
+            pltpu.SemaphoreType.DMA((total * count,)),
+            pltpu.SemaphoreType.DMA((count,)),
+        ],
+        compiler_params=pltpu.CompilerParams(
+            collective_id=collective_id, has_side_effects=True, vmem_limit_bytes=40 * 2 ** 20
+        ),
+        name="gather_pieces",
+    )(*pieces)
+
+
+def scatter_kernel(n_dp, n_fsdp, count, *refs):
+    parts, sums = refs[:count], refs[count : 2 * count]
+    rest = refs[2 * count :]
+    send_sem, recv_sem = rest[0], rest[1]
+    got_dp, got_w, got_a, got_u = (rest[2 + k * count : 2 + (k + 1) * count] for k in range(4))
+    put_w, put_a, put_u = (rest[2 + k * count : 2 + (k + 1) * count] for k in range(4, 7))
+    place = Place(n_dp, n_fsdp)
+    sender = Sender(place, send_sem)
+    lines = place.lines
+    base_w = (n_dp - 1) * n_fsdp
+    base_a = base_w + 2 * lines
+    base_u = base_a + 2 * (lines - 1)
+    place.greet()
+
+    def from_dp(dd, da, du, dw):
+        return (dd - 1) * n_fsdp + place.slot(0, da, du, dw)
+
+    def send(source, target, index, base, device):
+        for i in range(count):
+            sender.send(source(i), target[i].at[index], recv_sem.at[(base + index) * count + i], device)
+
+    def arrived(target, index, base):
+        for i in range(count):
+            sender.arrived(target[i].at[index], recv_sem.at[(base + index) * count + i])
+
+    order = [(da, du, dw) for dw in (1, 0) for da in list(range(1, lines)) + [0] for du in (1, 0)]
+    for da, du, dw in order:
+        for dd in range(1, n_dp):
+            piece = place.piece(dd, da, *((dw, du) if dd % 2 else (du, dw)))
+            send(lambda i: parts[i].at[piece], got_dp, from_dp(n_dp - dd, da, du, dw), 0, (dd, 0, 0, 0))
+
+    def total(i, da, du, dw, extra):
+        value = parts[i][place.piece(0, da, du, dw)].astype(F32)
+        for dd in range(1, n_dp):
+            value += got_dp[i][from_dp(dd, da, du, dw)].astype(F32)
+        for ref, index in extra:
+            value += ref[i][index].astype(F32)
+        return value
+
+    def await_dp(da, du, dw):
+        for dd in range(1, n_dp):
+            arrived(got_dp, from_dp(dd, da, du, dw), 0)
+
+    for da, du, dw in order:
+        await_dp(da, du, dw)
+        if dw == 1:
+            index = da * 2 + du
+            for i in range(count):
+                put_w[i][index] = total(i, da, du, 1, []).astype(BF16)
+            send(lambda i: put_w[i].at[index], got_w, index, base_w, (0, 0, 0, 1))
+    for da in list(range(1, lines)) + [0]:
+        for du in (1, 0):
+            extra = [(got_w, da * 2 + du)]
+            arrived(got_w, da * 2 + du, base_w)
+            if da:
+                index = (da - 1) * 2 + du
+                for i in range(count):
+                    put_a[i][index] = total(i, da, du, 0, extra).astype(BF16)
+                send(lambda i: put_a[i].at[index], got_a, (lines - da - 1) * 2 + du, base_a, (0, da, 0, 0))
+                continue
+            for k in range(lines - 1):
+                arrived(got_a, k * 2 + du, base_a)
+                extra.append((got_a, k * 2 + du))
+            if du:
+                for i in range(count):
+                    put_u[i][0] = total(i, 0, 1, 0, extra).astype(BF16)
+                send(lambda i: put_u[i].at[0], got_u, 0, base_u, (0, 0, 1, 0))
+            else:
+                arrived(got_u, 0, base_u)
+                extra.append((got_u, 0))
+                for i in range(count):
+                    sums[i][...] = total(i, 0, 0, 0, extra)
+    sender.drain()
+
+
+def scatter_sums(parts, n_dp, n_fsdp, collective_id):
+    count, lines = len(parts), n_fsdp // 4
+    copies = ((n_dp - 1) * n_fsdp + 2 * lines + 2 * (lines - 1) + 1) * count
+    sizes = [(n_dp - 1) * n_fsdp, 2 * lines, 2 * (lines - 1), 1, 2 * lines, 2 * (lines - 1), 1]
+    buffers = [pltpu.VMEM((size,) + part.shape[1:], BF16) for size in sizes for part in parts]
+    return pl.pallas_call(
+        partial(scatter_kernel, n_dp, n_fsdp, count),
+        in_specs=[pl.BlockSpec(memory_space=pltpu.VMEM)] * count,
+        out_specs=[pl.BlockSpec(memory_space=pltpu.VMEM)] * count,
+        out_shape=[jax.ShapeDtypeStruct(part.shape[1:], F32) for part in parts],
+        scratch_shapes=[pltpu.SemaphoreType.DMA((copies,)), pltpu.SemaphoreType.DMA((copies,))] + buffers,
+        compiler_params=pltpu.CompilerParams(
+            collective_id=collective_id, has_side_effects=True, vmem_limit_bytes=60 * 2 ** 20
+        ),
+        name="scatter_sums",
+    )(*parts)
+
+
 D = 768
 FF = 3072
 
@@ -252,12 +484,14 @@
     low_qkv, low_merge, low_expand, low_shrink, low_small = lowered
     axes = ("dp", "fsdp")
     own_rows = qkv_weight.shape[0]
-    first = jnp.concatenate([low_qkv, low_small.reshape(own_rows, -1)], axis=1)
-    first = lax.all_gather(first, axes, axis=0, tiled=True)
+    n_dp, n_fsdp = lax.axis_size("dp"), lax.axis_size("fsdp")
+    small_rows = jnp.pad(low_small.reshape(own_rows, -1), ((0, 0), (0, 128 - 8 - FF // D)))
+    qkv_full, small_full = gather_pieces([low_qkv, small_rows], n_dp, n_fsdp, 0)
+    qkv_full = qkv_full.reshape(D, 3 * D)
+    small_full = small_full.reshape(D, 128)[:, : 8 + FF // D]
     second = jnp.concatenate([low_merge, low_expand], axis=1)
     second = lax.all_gather(second, axes, axis=0, tiled=True)
     shrink_full = lax.all_gather(low_shrink, axes, axis=0, tiled=True)
-    qkv_full, small_full = first[:, : 3 * D], first[:, 3 * D :]
     merge_full, expand_full = second[:, :D], second[:, D:]
     pieces, bias_expand = split_vectors(small_full)
     gain_one, shift_one, bias_query, bias_value, bias_merge, gain_two, shift_two, bias_shrink = (
@@ -340,16 +574,17 @@
     all_rows = jnp.concatenate([vector_rows, expand_bias_part.reshape(FF // D, D)], axis=0)
     small_part = all_rows.T
     wide_part = jnp.concatenate([merge_part, expand_part], axis=1).astype(BF16)
-    last_part = jnp.concatenate([qkv_part, small_part], axis=1).astype(BF16)
     shrink_sum = lax.psum_scatter(shrink_part.astype(BF16), axes, scatter_dimension=0, tiled=True)
     wide_sum = lax.psum_scatter(wide_part, axes, scatter_dimension=0, tiled=True).astype(F32)
-    last_sum = lax.psum_scatter(last_part, axes, scatter_dimension=0, tiled=True).astype(F32)
+    small_part = jnp.pad(small_part, ((0, 0), (0, 128 - 8 - FF // D)))
+    last_parts = [part.astype(BF16).reshape(n_dp * n_fsdp, own_rows, -1) for part in (qkv_part, small_part)]
+    qkv_sum, small_sum = scatter_sums(last_parts, n_dp, n_fsdp, 1)
     summed = (
-        last_sum[:, : 3 * D],
+        qkv_sum,
         wide_sum[:, :D],
         wide_sum[:, D:],
         shrink_sum.astype(F32),
-        last_sum[:, 3 * D :].reshape(-1),
+        small_sum[:, : 8 + FF // D].reshape(-1),
     )
     rate_scale = (tokens.shape[0] * lax.axis_size("dp") * lax.axis_size("fsdp")) ** (-0.5)
     rates = (

time: 761 us -> 630 us (0.83)
  waiting for transfers between devices: 410 us -> 214 us
  Pallas kernels: 121 us -> 189 us
    reduce_scatter x1, waiting for transfers between devices: 113 us -> 34 us  [per_device(): lax.psum_scatter(wide_part, axes, scatter_dimension=0, tiled=True)]
    pallas_call x0 -> x2, Pallas kernels: none -> 68.3 us  [the longest x1 35.5 us: gather_pieces(): pl.pallas_call(partial(gather_kernel, n_dp, n_fsdp, count), in_specs=[pl....]
    all_gather x1 -> x0, waiting for transfers between devices: 58.7 us -> none  [per_device(): first = lax.all_gather(first, axes, axis=0, tiled=True)]
    unnamed x7 -> x4, waiting for transfers between devices: 55.8 us -> 0.07 us
    all_gather x1, waiting for transfers between devices: 13 us -> 0.01 us  [per_device(): second = lax.all_gather(second, axes, axis=0, tiled=True)]
    reduce_scatter x1, waiting for transfers between devices: 106 us -> 117 us  [per_device(): lax.psum_scatter(shrink_part.astype(BF16), axes, scatter_dimension=0, til...]
  transfers between devices with their start and end apart: 6 -> 4, of which waited for: 6 -> 3; matrix products, arithmetic and copies ran while one was open for 8% -> 11% of each run, Pallas kernels for 6% -> 18%
where the time goes in v2:
time: 630 us; the launch traced here: 622 us
  waiting for transfers between devices  214 us (34%)
  Pallas kernels  189 us (30%)
  matrix products  143 us (23%)
  other arithmetic  39.2 us (6%)
  local copies, waits for them, and re-layouts  22.4 us (4%)
  between operations  14.6 us (2%)
    reduce_scatter x1, waiting for transfers between devices, per_device(): lax.psum_scatter(shrink_part.astype(BF16), axes, scatter_dimension=0, til...  117 us
    pallas_call x1, Pallas kernels, attention_backward(): pl.pallas_call(partial(backward_kernel, slots, block), grid=(pairs,), in_...  75.5 us
    all_gather x1, waiting for transfers between devices, per_device(): shrink_full = lax.all_gather(low_shrink, axes, axis=0, tiled=True)  62.3 us
    dot_general x1, matrix products, per_device(): jnp.dot(norm_two_low, expand_full, preferred_element_type=jnp.float32)  49.3 us
    pallas_call x1, Pallas kernels, attention_forward(): pl.pallas_call(partial(forward_kernel, slots, block), grid=(pairs,), in_s...  44.9 us
    pallas_call x1, Pallas kernels, gather_pieces(): pl.pallas_call(partial(gather_kernel, n_dp, n_fsdp, count), in_specs=[pl....  35.5 us
    reduce_scatter x1, waiting for transfers between devices, per_device(): lax.psum_scatter(wide_part, axes, scatter_dimension=0, tiled=True)  34 us
    pallas_call x1, Pallas kernels, scatter_sums(): pl.pallas_call(partial(scatter_kernel, n_dp, n_fsdp, count), in_specs=[pl...  32.8 us
  transfers between devices with their start and end apart: 4, of which 3 were waited for; matrix products, arithmetic and copies ran while one was open for 11% of the time, Pallas kernels for 18%

profile of v2, /device:TPU:0, one launch (start us, length us, event | category | flops | bytes accessed | tf_op | source)
XLA Modules:
  0.0 621.7 jit_solution(9704921525979365429)
XLA Ops:
  7.2 1.0 convert_element_type.112
  8.2 0.9 convert_element_type.111
  9.1 0.7 pad_maximum_fusion.1
  9.9 1.0 convert_element_type.104.refs_0_
  10.8 0.7 convert_element_type.105
  11.6 35.5 %gather_pieces.1 = (bf16[32,24,2304]{2,1,0:T(8,128)(2,1)S(1)}, bf16[32,24,128]{2,1,0:T(8,128)(2,1)S(1)}) custom-call(bf16[24,2304]{1,0:T(8,128)(2,1)S(1)} %convert_element_type.104.refs_0_, bf16[24,128]{1,0:T(8,128)(2,1)S(1)} %pad.10.refs_1_), custom_call_target="tpu_custom_call" | custom-call | tf_op jit(solution)/shard_map/gather_pieces/pallas_call | solution.py:322
  47.2 1.8 copy-done.2
  49.0 0.7 copy.50
  49.7 0.9 convert_element_type.106
  50.6 0.6 copy-done.30
  51.2 0.6 add.182
  51.8 0.8 fusion.57
  52.6 1.8 slice_reduce_fusion
  54.5 1.8 convert_reduce_fusion
  56.3 2.2 fusion.36
  58.5 0.3 select_convert_fusion
  58.8 9.5 %fusion.16.q_ref.k_ref.v_ref = bf16[1190,2304]{1,0:T(8,128)(2,1)} fusion(bf16[768,2304]{1,0:T(8,128)(2,1)S(1)} %bitcast.22, f32[2304]{0:T(1024)S(1)} %pad_maximum_fusion.2, bf16[1190,768]{1,0:T(8,128)(2,1)} %param.19, f32[768]{0:T(1024)S(1)} %get-tuple-element.61, f32[768]{0:T(1024)S(1)} %get-tuple-element.62, f32[1190]{0:T(1024)S(1)} %add_rsqrt_fusion.1, ...), kind=kOutput, calls=%fused_computation.27 | convolution fusion | flops 4222310400 | bytes 10875184 | tf_op jit(solution)/shard_map/dot_general | solution.py:504
  68.3 44.9 %attention_forward.1 = (bf16[1190,768]{1,0:T(8,128)(2,1)S(1)}, f32[1190,768]{1,0:T(8,128)}, f32[1190,768]{1,0:T(8,128)}) custom-call(bf16[1190,2304]{1,0:T(8,128)(2,1)} %fusion.16.q_ref.k_ref.v_ref, bf16[1190,2304]{1,0:T(8,128)(2,1)} %fusion.16.q_ref.k_ref.v_ref, bf16[1190,2304]{1,0:T(8,128)(2,1)} %fusion.16.q_ref.k_ref.v_ref, ...), custom_call_target="tpu_custom_call" | custom-call | tf_op jit(solution)/shard_map/attention_forward/pallas_call | solution.py:100
  113.3 4.4 fusion.59
  117.7 0.6 multiply_reduce_fusion.2
  118.3 0.1 copy-done.40
  118.4 49.3 %fusion.2 = (bf16[1190,3072]{1,0:T(8,128)(2,1)S(1)}, f32[1190,3072]{1,0:T(8,128)}) fusion(f32[3072]{0:T(1024)S(1)} %copy-done.40, bf16[768,3840]{1,0:T(8,128)(2,1)S(1)} %bitcast.29, f32[1190,768]{1,0:T(8,128)S(1)} %get-tuple-element.91, f32[768]{0:T(1024)S(1)} %get-tuple-element.56, f32[768]{0:T(1024)S(1)} %get-tuple-element.57, ...), kind=kOutput, calls=%fused_computation.4 | convolution fusion | flops 5860968960 | bytes 30351360 | tf_op jit(solution)/shard_map/dot_general | solution.py:513
  167.7 2.9 copy-done.54
  170.7 8.8 %convolution_convert_fusion.1 = bf16[3072,768]{1,0:T(8,128)(2,1)} fusion(bf16[1190,3072]{1,0:T(8,128)(2,1)S(1)} %get-tuple-element.92, bf16[1190,768]{1,0:T(8,128)(2,1)S(1)} %copy-done.12, f32[1190]{0:T(1024)S(1)} %get-tuple-element.86), kind=kOutput, calls=%fused_computation.33 | convolution fusion | flops 5620225536 | bytes 13862552 | tf_op jit(solution)/shard_map/sf,sd->fd/dot_general | solution.py:522
  179.5 117.2 %reduce-scatter.5.cloned.1.call-done = bf16[96,768]{1,0:T(8,128)(2,1)} async-done(((bf16[3072,768]{1,0:T(8,128)(2,1)}), bf16[96,768]{1,0:T(8,128)(2,1)}) %reduce-scatter.5.cloned.1.call-update) | async-done | bytes 147472 | tf_op jit(solution)/shard_map/reduce_scatter | solution.py:577
  296.7 1.9 fusion.53
  298.7 0.4 fusion.37
  299.1 0.6 stack.39
  299.7 0.7 add_multiply_fusion
  300.4 62.3 %all-gather.5.cloned.1.call-done = bf16[3072,768]{1,0:T(8,128)(2,1)} async-done(((bf16[96,768]{1,0:T(8,128)(2,1)}), bf16[3072,768]{1,0:T(8,128)(2,1)}) %all-gather.5.cloned.1.call-update) | async-done | bytes 4718608 | tf_op jit(solution)/shard_map/all_gather | solution.py:494
  362.7 14.4 %fusion.60 = (bf16[3072]{0:T(1024)(128)(2,1)}, bf16[1190,3072]{1,0:T(8,128)(2,1)S(1)}) fusion(f32[1190,3072]{1,0:T(8,128)} %get-tuple-element.93, f32[3072]{0:T(1024)S(1)} %copy-done.40, bf16[3072,768]{1,0:T(8,128)(2,1)} %all-gather.5.cloned.1.call-done, bf16[1190,768]{1,0:T(8,128)(2,1)S(1)} %copy-done.12, f32[1190]{0:T(1024)S(1)} %get-tuple-element.86), kind=kOutput, calls=%fused_computation.134 | convolution fusion | flops 5661731328 | bytes 28503704 | tf_op jit(solution)/shard_map/sd,fd->sf/dot_general | solution.py:526
  377.1 8.7 %convolution_convert_fusion.2 = bf16[768,3072]{1,0:T(8,128)(2,1)} fusion(bf16[1190,3072]{1,0:T(8,128)(2,1)S(1)} %get-tuple-element.97, f32[1190,768]{1,0:T(8,128)S(1)} %copy-done.9, f32[768]{0:T(1024)S(1)} %get-tuple-element.56, f32[768]{0:T(1024)S(1)} %get-tuple-element.57, f32[1190]{0:T(1024)S(1)} %add_rsqrt_fusion, f32[1190]{0:T(1024)S(1)} %broadcast_multiply_fusion.4), kind=kOutput, calls=%fused_computation.34 | convolution fusion | flops 5622053376 | bytes 15701296 | tf_op jit(solution)/shard_map/sd,sf->df/dot_general | solution.py:532
  385.8 10.1 %multiply_reduce_fusion = (bf16[768]{0:T(1024)(128)(2,1)}, f32[1190]{0:T(1024)S(1)}, f32[1190]{0:T(1024)S(1)}, bf16[768]{0:T(1024)(128)(2,1)}, f32[1190,768]{1,0:T(8,128)S(1)}) fusion(f32[1190,768]{1,0:T(8,128)S(1)} %copy-done.9, f32[1190]{0:T(1024)S(1)} %add_rsqrt_fusion, f32[1190]{0:T(1024)S(1)} %broadcast_multiply_fusion.4, ...), kind=kOutput, calls=%fused_computation.56 | convolution fusion | flops 5623346176 | bytes 19366496 | tf_op jit(solution)/shard_map/sf,df->sd/dot_general | solution.py:536
  395.9 2.4 convert_reduce_fusion.1
  398.3 1.9 convolution_convert_fusion.4
  400.2 4.2 convolution_convert_fusion.3.g_ref
  404.4 75.5 %attention_backward.1 = (bf16[1190,768]{1,0:T(8,128)(2,1)}, bf16[1190,768]{1,0:T(8,128)(2,1)}, bf16[1190,768]{1,0:T(8,128)(2,1)}) custom-call(bf16[1190,2304]{1,0:T(8,128)(2,1)} %fusion.16.q_ref.k_ref.v_ref, bf16[1190,2304]{1,0:T(8,128)(2,1)} %fusion.16.q_ref.k_ref.v_ref, bf16[1190,2304]{1,0:T(8,128)(2,1)} %fusion.16.q_ref.k_ref.v_ref, ...), custom_call_target="tpu_custom_call" | custom-call | tf_op jit(solution)/shard_map/attention_backward/pallas_call | solution.py:186
  479.9 3.0 constant_dynamic-update-slice_fusion.2
  482.9 1.4 constant_dynamic-update-slice_fusion.1
  484.3 1.4 constant_dynamic-update-slice_fusion
  485.7 4.0 reduce
  489.7 1.0 copy.49
  490.7 5.3 pad_maximum_fusion
  496.0 2.0 copy-done.4
  498.0 11.0 %fusion.35 = (bf16[768]{0:T(1024)(128)(2,1)S(1)}, f32[1190]{0:T(1024)}, f32[1190]{0:T(1024)}, bf16[768]{0:T(1024)(128)(2,1)S(1)}, f32[1190,768]{1,0:T(8,128)}) fusion(bf16[1190,768]{1,0:T(8,128)(2,1)} %param.19, f32[1190]{0:T(1024)S(1)} %copy-done.36, f32[1190]{0:T(1024)S(1)} %copy-done.34, f32[768]{0:T(1024)} %copy-done.38, ...), kind=kOutput, calls=%fused_computation.54 | convolution fusion | flops 4220478464 | bytes 14531168 | tf_op jit(solution)/shard_map/sc,dc->sd/dot_general | solution.py:557
  509.1 0.7 reshape.131
  509.8 0.7 concatenate.24
  510.6 0.2 copy.51
  510.8 0.7 pad.11.clone
  511.5 10.3 %convolution_convert_fusion = bf16[768,2304]{1,0:T(8,128)(2,1)} fusion(bf16[1190,2304]{1,0:T(8,128)(2,1)} %constant_dynamic-update-slice_fusion, bf16[1190,768]{1,0:T(8,128)(2,1)} %param.19, f32[768]{0:T(1024)} %copy-done.48, f32[768]{0:T(1024)} %copy-done.38, f32[1190]{0:T(1024)S(1)} %copy-done.36, f32[1190]{0:T(1024)S(1)} %copy-done.34), kind=kOutput, calls=%fused_computation.32 | convolution fusion | flops 4218596352 | bytes 10865968 | tf_op jit(solution)/shard_map/sd,sc->dc/dot_general | solution.py:553
  521.9 32.8 %scatter_sums.1 = (f32[24,2304]{1,0:T(8,128)}, f32[24,128]{1,0:T(8,128)}) custom-call(bf16[32,24,2304]{2,1,0:T(8,128)(2,1)} %bitcast.24, bf16[32,24,128]{2,1,0:T(8,128)(2,1)} %bitcast.25), custom_call_target="tpu_custom_call" | custom-call | tf_op jit(solution)/shard_map/scatter_sums/pallas_call | solution.py:419
  554.6 1.0 reshape.133
  555.6 0.6 fusion.52
  556.2 0.6 add_multiply_fusion.4
  556.9 1.7 fusion.56
  558.6 0.8 add_multiply_fusion.2
  559.3 5.4 fusion.34
  564.9 10.6 %fusion.39 = bf16[1190,768]{1,0:T(8,128)(2,1)} fusion(f32[1190,768]{1,0:T(8,128)S(1)} %copy-done.10, bf16[1190,3072]{1,0:T(8,128)(2,1)} %copy-done.54, bf16[3072,768]{1,0:T(8,128)(2,1)} %all-gather.5.cloned.1.call-done, f32[768]{0:T(1024)S(1)} %copy-done.47), kind=kOutput, calls=%fused_computation.65 | convolution fusion | flops 5617866240 | bytes 17516544 | tf_op jit(solution)/shard_map/dot_general | solution.py:516
  575.5 34.0 %reduce-scatter.3.cloned.1.call-done = bf16[24,3840]{1,0:T(8,128)(2,1)} async-done(((bf16[768,3840]{1,0:T(8,128)(2,1)}), bf16[24,3840]{1,0:T(8,128)(2,1)}) %reduce-scatter.3.cloned.1.call-update) | async-done | bytes 184336 | tf_op jit(solution)/shard_map/reduce_scatter | solution.py:578
  609.5 1.4 fusion.55
  611.0 0.7 add_multiply_fusion.3
  611.6 1.8 fusion.54
  613.5 0.8 add_multiply_fusion.1
  614.3 0.7 copy.55
  (143 shorter events, 0.7 us)
Async XLA Ops:
  7.2 106.1 %all-gather.3.cloned.1.call-start = ((), (), s32[]{:S(2)}) async-start(), calls=%async_computation.2 | async-start | bytes 6082560 | tf_op jit(solution)/shard_map/all_gather | solution.py:493
  9.8 286.9 %reduce-scatter.5.cloned.1.call-start = ((), (), s32[]{:S(2)}) async-start(), calls=%async_computation.5 | async-start | bytes 4866048 | tf_op jit(solution)/shard_map/reduce_scatter | solution.py:577
  47.2 1.8 copy-start.2
  49.7 9.1 %copy-start.3 = (bf16[32,24,2304]{2,1,0:T(8,128)(2,1)S(1)}, bf16[32,24,2304]{2,1,0:T(8,128)(2,1)}, u32[]{:S(2)}) copy-start(bf16[32,24,2304]{2,1,0:T(8,128)(2,1)} %copy-done.2) | copy-start | bytes 10616836
  50.6 0.6 copy-start.30
  54.4 13.9 %copy-start.38 = (f32[768]{0:T(1024)}, f32[768]{0:T(1024)S(1)}, u32[]{:S(2)}) copy-start(f32[768]{0:T(1024)S(1)} %get-tuple-element.62) | copy-start | bytes 9220
  54.4 13.9 %copy-start.48 = (f32[768]{0:T(1024)}, f32[768]{0:T(1024)S(1)}, u32[]{:S(2)}) copy-start(f32[768]{0:T(1024)S(1)} %get-tuple-element.61) | copy-start | bytes 9220
  56.3 12.0 %copy-start.33 = (f32[1190]{0:T(1024)}, f32[1190]{0:T(1024)S(1)}, u32[]{:S(2)}) copy-start(f32[1190]{0:T(1024)S(1)} %broadcast_multiply_fusion.5) | copy-start | bytes 14284
  58.5 9.8 %copy-start.35 = (f32[1190]{0:T(1024)}, f32[1190]{0:T(1024)S(1)}, u32[]{:S(2)}) copy-start(f32[1190]{0:T(1024)S(1)} %add_rsqrt_fusion.1) | copy-start | bytes 14284
  58.8 9.5 %copy-start = (bf16[1280,128]{1,0:T(8,128)(2,1)}, bf16[1280,128]{1,0:T(8,128)(2,1)S(1)}, u32[]{:S(2)}) copy-start(bf16[1280,128]{1,0:T(8,128)(2,1)S(1)} %get-tuple-element.84.fk_ref) | copy-start | bytes 983044
  58.8 9.5 %copy-start.1 = (bf16[1280,128]{1,0:T(8,128)(2,1)}, bf16[1280,128]{1,0:T(8,128)(2,1)S(1)}, u32[]{:S(2)}) copy-start(bf16[1280,128]{1,0:T(8,128)(2,1)S(1)} %get-tuple-element.85.fq_ref) | copy-start | bytes 983044
  68.3 45.0 %copy-start.49 = (f32[768]{0:T(1024)S(1)}, f32[768]{0:T(1024)}, u32[]{:S(2)}) copy-start(f32[768]{0:T(1024)} %get-tuple-element.58) | copy-start | bytes 9220
  113.3 4.4 copy-start.5
  113.3 5.0 slice-start
  113.3 5.0 slice-start.1
  117.7 50.0 %copy-start.8 = (f32[1190,768]{1,0:T(8,128)}, f32[1190,768]{1,0:T(8,128)S(1)}, u32[]{:S(2)}) copy-start(f32[1190,768]{1,0:T(8,128)S(1)} %get-tuple-element.91) | copy-start | bytes 10967044
  117.7 0.7 copy-start.40
  118.4 52.2 %copy-start.12 = (bf16[1190,768]{1,0:T(8,128)(2,1)S(1)}, bf16[1190,768]{1,0:T(8,128)(2,1)}, u32[]{:S(2)}) copy-start(bf16[1190,768]{1,0:T(8,128)(2,1)} %param.20) | copy-start | bytes 5483524
  167.7 2.9 copy-start.54
  179.4 117.3 %copy-start.25 = (f32[96,768]{1,0:T(8,128)S(1)}, f32[96,768]{1,0:T(8,128)}, u32[]{:S(2)}) copy-start(f32[96,768]{1,0:T(8,128)} %param.32) | copy-start | bytes 884740
  179.4 117.3 %copy-start.26 = (f32[96,768]{1,0:T(8,128)S(1)}, f32[96,768]{1,0:T(8,128)}, u32[]{:S(2)}) copy-start(f32[96,768]{1,0:T(8,128)} %param.33) | copy-start | bytes 884740
  179.4 120.3 %copy-start.21 = (f32[96,768]{1,0:T(8,128)S(1)}, f32[96,768]{1,0:T(8,128)}, u32[]{:S(2)}) copy-start(f32[96,768]{1,0:T(8,128)} %param.34) | copy-start | bytes 884740
  179.5 183.2 %all-gather.5.cloned.1.call-start = ((), (), s32[]{:S(2)}) async-start(), calls=%async_computation.3 | async-start | bytes 4866048 | tf_op jit(solution)/shard_map/all_gather | solution.py:494
  298.6 78.5 %copy-start.15 = (f32[96,768]{1,0:T(8,128)}, f32[96,768]{1,0:T(8,128)S(1)}, u32[]{:S(2)}) copy-start(f32[96,768]{1,0:T(8,128)S(1)} %get-tuple-element.146) | copy-start | bytes 884740
  298.6 310.9 %reduce-scatter.3.cloned.1.call-start = ((), (), s32[]{:S(2)}) async-start(), calls=%async_computation.4 | async-start | bytes 6082560 | tf_op jit(solution)/shard_map/reduce_scatter | solution.py:578
  362.7 14.4 %copy-start.9 = (f32[1190,768]{1,0:T(8,128)S(1)}, f32[1190,768]{1,0:T(8,128)}, u32[]{:S(2)}) copy-start(f32[1190,768]{1,0:T(8,128)} %copy-done.8) | copy-start | bytes 10967044
  395.9 2.4 copy-start.6
  398.3 1.9 copy-start.11
  479.9 3.0 copy-start.14
  479.9 4.4 copy-start.13
  496.0 2.0 copy-start.4
  496.0 2.0 copy-start.34
  496.0 2.0 copy-start.36
  498.0 11.0 %copy-start.37 = (bf16[2304]{0:T(1024)(128)(2,1)S(1)}, bf16[2304]{0:T(1024)(128)(2,1)}, u32[]{:S(2)}) copy-start(bf16[2304]{0:T(1024)(128)(2,1)} %reduce) | copy-start | bytes 13828
  498.0 11.1 %copy-start.46 = (bf16[768]{0:T(1024)(128)(2,1)S(1)}, bf16[768]{0:T(1024)(128)(2,1)}, u32[]{:S(2)}) copy-start(bf16[768]{0:T(1024)(128)(2,1)} %get-tuple-element.81) | copy-start | bytes 4612
  498.0 11.1 %copy-start.52 = (bf16[768]{0:T(1024)(128)(2,1)S(1)}, bf16[768]{0:T(1024)(128)(2,1)}, u32[]{:S(2)}) copy-start(bf16[768]{0:T(1024)(128)(2,1)} %get-tuple-element.47) | copy-start | bytes 4612
  498.0 11.1 %copy-start.51 = (bf16[768]{0:T(1024)(128)(2,1)S(1)}, bf16[768]{0:T(1024)(128)(2,1)}, u32[]{:S(2)}) copy-start(bf16[768]{0:T(1024)(128)(2,1)} %get-tuple-element.53) | copy-start | bytes 4612
  521.8 33.8 %copy-start.45 = (f32[288]{0:T(512)S(1)}, f32[288]{0:T(512)}, u32[]{:S(2)}) copy-start(f32[288]{0:T(512)} %param.35) | copy-start | bytes 3460
  521.8 33.9 %copy-start.53 = (f32[288]{0:T(512)S(1)}, f32[288]{0:T(512)}, u32[]{:S(2)}) copy-start(f32[288]{0:T(512)} %param.36) | copy-start | bytes 3460
  521.8 34.5 %copy-start.50 = (f32[288]{0:T(512)S(1)}, f32[288]{0:T(512)}, u32[]{:S(2)}) copy-start(f32[288]{0:T(512)} %param.37) | copy-start | bytes 3460
  521.8 35.0 %copy-start.42 = (f32[1190]{0:T(1024)S(1)}, f32[1190]{0:T(1024)}, u32[]{:S(2)}) copy-start(f32[1190]{0:T(1024)} %get-tuple-element.50) | copy-start | bytes 14284
  521.8 35.0 %copy-start.41 = (f32[1190]{0:T(1024)S(1)}, f32[1190]{0:T(1024)}, u32[]{:S(2)}) copy-start(f32[1190]{0:T(1024)} %get-tuple-element.51) | copy-start | bytes 14284
  521.8 35.0 %copy-start.19 = (f32[24,2304]{1,0:T(8,128)S(1)}, f32[24,2304]{1,0:T(8,128)}, u32[]{:S(2)}) copy-start(f32[24,2304]{1,0:T(8,128)} %param.23) | copy-start | bytes 663556
  521.8 35.0 %copy-start.28 = (f32[24,2304]{1,0:T(8,128)S(1)}, f32[24,2304]{1,0:T(8,128)}, u32[]{:S(2)}) copy-start(f32[24,2304]{1,0:T(8,128)} %param.24) | copy-start | bytes 663556
  521.8 36.7 %copy-start.29 = (f32[24,2304]{1,0:T(8,128)S(1)}, f32[24,2304]{1,0:T(8,128)}, u32[]{:S(2)}) copy-start(f32[24,2304]{1,0:T(8,128)} %param.25) | copy-start | bytes 663556
  521.8 37.5 %copy-start.7 = (bf16[1190,768]{1,0:T(8,128)(2,1)S(1)}, bf16[1190,768]{1,0:T(8,128)(2,1)}, u32[]{:S(2)}) copy-start(bf16[1190,768]{1,0:T(8,128)(2,1)} %param.19) | copy-start | bytes 5483524
  521.8 37.5 %copy-start.39 = (f32[768]{0:T(1024)S(1)}, f32[768]{0:T(1024)}, u32[]{:S(2)}) copy-start(f32[768]{0:T(1024)} %copy-done.38) | copy-start | bytes 9220
  555.6 9.1 %copy-start.43 = (f32[288]{0:T(512)}, f32[288]{0:T(512)S(1)}, u32[]{:S(2)}) copy-start(f32[288]{0:T(512)S(1)} %reshape.133) | copy-start | bytes 3460
  556.2 8.5 %copy-start.44 = (f32[288]{0:T(512)}, f32[288]{0:T(512)S(1)}, u32[]{:S(2)}) copy-start(f32[288]{0:T(512)S(1)} %get-tuple-element.151) | copy-start | bytes 3460
  558.6 6.2 copy-start.20
  559.3 5.4 copy-start.10
  559.3 5.5 copy-start.47
  564.8 44.7 %copy-start.24 = (f32[24,768]{1,0:T(8,128)S(1)}, f32[24,768]{1,0:T(8,128)}, u32[]{:S(2)}) copy-start(f32[24,768]{1,0:T(8,128)} %param.26) | copy-start | bytes 221188
  564.8 44.7 %copy-start.32 = (f32[24,768]{1,0:T(8,128)S(1)}, f32[24,768]{1,0:T(8,128)}, u32[]{:S(2)}) copy-start(f32[24,768]{1,0:T(8,128)} %param.27) | copy-start | bytes 221188
  564.8 46.2 %copy-start.31 = (f32[24,768]{1,0:T(8,128)S(1)}, f32[24,768]{1,0:T(8,128)}, u32[]{:S(2)}) copy-start(f32[24,768]{1,0:T(8,128)} %param.28) | copy-start | bytes 221188
  564.8 46.8 %copy-start.17 = (f32[24,3072]{1,0:T(8,128)S(1)}, f32[24,3072]{1,0:T(8,128)}, u32[]{:S(2)}) copy-start(f32[24,3072]{1,0:T(8,128)} %param.29) | copy-start | bytes 884740
  564.8 46.8 %copy-start.27 = (f32[24,3072]{1,0:T(8,128)S(1)}, f32[24,3072]{1,0:T(8,128)}, u32[]{:S(2)}) copy-start(f32[24,3072]{1,0:T(8,128)} %param.30) | copy-start | bytes 884740
  564.8 48.6 %copy-start.22 = (f32[24,3072]{1,0:T(8,128)S(1)}, f32[24,3072]{1,0:T(8,128)}, u32[]{:S(2)}) copy-start(f32[24,3072]{1,0:T(8,128)} %param.31) | copy-start | bytes 884740
  575.5 38.8 %copy-start.18 = (f32[24,2304]{1,0:T(8,128)S(1)}, f32[24,2304]{1,0:T(8,128)}, u32[]{:S(2)}) copy-start(f32[24,2304]{1,0:T(8,128)} %get-tuple-element.129) | copy-start | bytes 663556
  611.0 4.0 copy-start.23
  613.5 1.5 copy-start.16
Sparse Core Ops, SparseCore 0:
  11.5 75.7 all-gather.2
  179.6 117.0 reduce-scatter.4
  300.2 62.4 all-gather.4
  496.2 113.3 reduce-scatter.2

commit v3 on v2

--- a/solution.py
+++ b/solution.py
@@ -197,6 +197,43 @@
     )(qkv, qkv, qkv, upstream, wide_out, lse, fq, fk)
 
 
+root_half = 0.7071067811865476
+inverse_root_tau = 0.3989422804014327
+
+
+def expand_kernel(chunk, x_ref, w_ref, b_ref, after_ref, slope_ref):
+    x = x_ref[...]
+
+    def step(number, carry):
+        cols = pl.ds(pl.multiple_of(number * chunk, 128), chunk)
+        before = dot_nn(x, w_ref[:, cols]) + b_ref[:, cols]
+        cumulative = 0.5 * (1.0 + lax.erf(before * root_half))
+        density = jnp.exp(-0.5 * before * before) * inverse_root_tau
+        after_ref[:, cols] = (before * cumulative).astype(BF16)
+        slope_ref[:, cols] = (cumulative + before * density).astype(BF16)
+        return carry
+
+    lax.fori_loop(0, w_ref.shape[1] // chunk, step, 0)
+
+
+def expand_forward(x, weight, bias, block=240, chunk=768):
+    slots, inner = x.shape
+    hidden = weight.shape[1]
+    return pl.pallas_call(
+        partial(expand_kernel, chunk),
+        grid=(round_up(slots, block) // block,),
+        in_specs=[
+            pl.BlockSpec((block, inner), lambda r: (r, 0)),
+            pl.BlockSpec((inner, hidden), lambda r: (0, 0)),
+            pl.BlockSpec((1, hidden), lambda r: (0, 0)),
+        ],
+        out_specs=[pl.BlockSpec((block, hidden), lambda r: (r, 0))] * 2,
+        out_shape=[jax.ShapeDtypeStruct((slots, hidden), BF16)] * 2,
+        compiler_params=pltpu.CompilerParams(vmem_limit_bytes=40 * 2 ** 20),
+        name="expand_forward",
+    )(x, weight, bias.reshape(1, -1))
+
+
 MESH = pl.DeviceIdType.MESH
 
 
@@ -434,8 +471,6 @@
 
 
 epsilon = 1e-06
-root_half = 0.7071067811865476
-inverse_root_tau = 0.3989422804014327
 
 
 def normalize_keep(values, gain_vector, shift_vector):
@@ -510,8 +545,7 @@
     )
     norm_two, scaled_two, inverse_two = normalize_keep(middle, gain_two, shift_two)
     norm_two_low = norm_two.astype(jnp.bfloat16)
-    before = jnp.dot(norm_two_low, expand_full, preferred_element_type=jnp.float32) + bias_expand
-    after_low = jax.nn.gelu(before, approximate=False).astype(jnp.bfloat16)
+    after_low, slope = expand_forward(norm_two_low, expand_full, bias_expand)
     output = (
         middle + jnp.dot(after_low, shrink_full, preferred_element_type=jnp.float32) + bias_shrink
     )
@@ -523,12 +557,11 @@
         "sf,sd->fd", after_low, outgoing_low, preferred_element_type=jnp.float32
     )
     shrink_bias_part = jnp.sum(outgoing, axis=0)
+    shrink_low, shrink_full = lax.optimization_barrier((shrink_part.astype(BF16), shrink_full))
     act_grad = jnp.einsum(
         "sd,fd->sf", outgoing_low, shrink_full, preferred_element_type=jnp.float32
     )
-    cumulative = 0.5 * (1.0 + lax.erf(before * root_half))
-    density = jnp.exp(-0.5 * before * before) * inverse_root_tau
-    before_grad = (act_grad * (cumulative + before * density)).astype(jnp.bfloat16)
+    before_grad = (act_grad * slope.astype(F32)).astype(BF16)
     expand_part = jnp.einsum(
         "sd,sf->df", norm_two_low, before_grad, preferred_element_type=jnp.float32
     )
@@ -574,7 +607,7 @@
     all_rows = jnp.concatenate([vector_rows, expand_bias_part.reshape(FF // D, D)], axis=0)
     small_part = all_rows.T
     wide_part = jnp.concatenate([merge_part, expand_part], axis=1).astype(BF16)
-    shrink_sum = lax.psum_scatter(shrink_part.astype(BF16), axes, scatter_dimension=0, tiled=True)
+    shrink_sum = lax.psum_scatter(shrink_low, axes, scatter_dimension=0, tiled=True)
     wide_sum = lax.psum_scatter(wide_part, axes, scatter_dimension=0, tiled=True).astype(F32)
     small_part = jnp.pad(small_part, ((0, 0), (0, 128 - 8 - FF // D)))
     last_parts = [part.astype(BF16).reshape(n_dp * n_fsdp, own_rows, -1) for part in (qkv_part, small_part)]

time: 630 us -> 426 us (0.68)
  waiting for transfers between devices: 214 us -> 34.6 us
  matrix products: 143 us -> 91.9 us
  Pallas kernels: 189 us -> 210 us
    reduce_scatter x1, waiting for transfers between devices: 117 us -> 0.01 us  [per_device(): lax.psum_scatter(shrink_low, axes, scatter_dimension=0, tiled=True)]
    all_gather x1, waiting for transfers between devices: 62.3 us -> 8.4 us  [per_device(): shrink_full = lax.all_gather(low_shrink, axes, axis=0, tiled=True)]
    dot_general x1 -> x0, matrix products: 49.3 us -> none  [per_device(): jnp.dot(norm_two_low, expand_full, preferred_element_type=jnp.float32)]
    pallas_call x0 -> x1, Pallas kernels: none -> 15.9 us  [expand_forward(): pl.pallas_call(partial(expand_kernel, chunk), grid=(round_up(slots, block...]
    reduce_scatter x1, waiting for transfers between devices: 34 us -> 26.2 us  [per_device(): lax.psum_scatter(wide_part, axes, scatter_dimension=0, tiled=True)]
    unnamed x119 -> x105, local copies, waits for them, and re-layouts: 13.6 us -> 16.6 us
  transfers between devices with their start and end apart: 4 -> 4, of which waited for: 3 -> 2; matrix products, arithmetic and copies ran while one was open for 11% -> 33% of each run, Pallas kernels for 18% -> 50%
where the time goes in v3:
time: 426 us; the launch traced here: 418 us
  Pallas kernels  210 us (49%)
  matrix products  91.9 us (22%)
  other arithmetic  40.7 us (10%)
  waiting for transfers between devices  34.6 us (8%)
  local copies, waits for them, and re-layouts  26.5 us (6%)
  between operations  14.6 us (3%)
    pallas_call x1, Pallas kernels, attention_backward(): pl.pallas_call(partial(backward_kernel, slots, block), grid=(pairs,), in_...  75.7 us
    pallas_call x1, Pallas kernels, attention_forward(): pl.pallas_call(partial(forward_kernel, slots, block), grid=(pairs,), in_s...  45 us
    pallas_call x1, Pallas kernels, scatter_sums(): pl.pallas_call(partial(scatter_kernel, n_dp, n_fsdp, count), in_specs=[pl...  37.4 us
    pallas_call x1, Pallas kernels, gather_pieces(): pl.pallas_call(partial(gather_kernel, n_dp, n_fsdp, count), in_specs=[pl....  35.5 us
    reduce_scatter x1, waiting for transfers between devices, per_device(): lax.psum_scatter(wide_part, axes, scatter_dimension=0, tiled=True)  26.2 us
    unnamed x105, local copies, waits for them, and re-layouts  16.6 us
    pallas_call x1, Pallas kernels, expand_forward(): pl.pallas_call(partial(expand_kernel, chunk), grid=(round_up(slots, block...  15.9 us
    dot_general x1, matrix products, per_device(): jnp.einsum('sf,df->sd', before_grad, expand_full, preferred_element_type=...  12.6 us
  transfers between devices with their start and end apart: 4, of which 2 were waited for; matrix products, arithmetic and copies ran while one was open for 33% of the time, Pallas kernels for 50%

profile of v3, /device:TPU:0, one launch (start us, length us, event | category | flops | bytes accessed | tf_op | source)
XLA Modules:
  0.0 418.0 jit_solution(8750726651870903035)
XLA Ops:
  7.3 1.1 convert_element_type.112
  8.4 0.9 convert_element_type.111
  9.3 0.7 pad_maximum_fusion.1
  10.0 1.6 convert_element_type.114
  11.7 1.0 convert_element_type.104.refs_0_
  12.7 0.7 convert_element_type.105
  13.5 35.5 %gather_pieces.1 = (bf16[32,24,2304]{2,1,0:T(8,128)(2,1)S(1)}, bf16[32,24,128]{2,1,0:T(8,128)(2,1)S(1)}) custom-call(bf16[24,2304]{1,0:T(8,128)(2,1)S(1)} %convert_element_type.104.refs_0_, bf16[24,128]{1,0:T(8,128)(2,1)S(1)} %pad.10.refs_1_), custom_call_target="tpu_custom_call" | custom-call | tf_op jit(solution)/shard_map/gather_pieces/pallas_call | solution.py:359
  49.1 1.8 copy-done.3
  50.8 0.1 copy.51
  51.0 0.9 fusion.39
  51.9 2.1 fusion.17
  54.0 0.6 stack.39
  54.6 0.6 slice_reduce_fusion
  55.3 0.3 convert_reduce_fusion
  55.6 0.7 fusion.16
  56.3 0.3 select_convert_fusion
  56.6 6.7 %fusion.q_ref.k_ref.v_ref = bf16[1190,2304]{1,0:T(8,128)(2,1)} fusion(bf16[768,2304]{1,0:T(8,128)(2,1)S(1)} %bitcast.29, f32[2304]{0:T(1024)S(1)} %pad_maximum_fusion.2, bf16[1190,768]{1,0:T(8,128)(2,1)S(1)} %copy-done.11, f32[768]{0:T(1024)S(1)} %get-tuple-element.69, f32[768]{0:T(1024)S(1)} %get-tuple-element.70, f32[1190]{0:T(1024)S(1)} %add_rsqrt_fusion.1, ...), kind=kOutput, calls=%fused_computation.2 | convolution fusion | flops 4222310400 | bytes 10875184 | tf_op jit(solution)/shard_map/dot_general | solution.py:539
  63.4 45.0 %attention_forward.1 = (bf16[1190,768]{1,0:T(8,128)(2,1)S(1)}, f32[1190,768]{1,0:T(8,128)}, f32[1190,768]{1,0:T(8,128)}) custom-call(bf16[1190,2304]{1,0:T(8,128)(2,1)} %fusion.q_ref.k_ref.v_ref, bf16[1190,2304]{1,0:T(8,128)(2,1)} %fusion.q_ref.k_ref.v_ref, bf16[1190,2304]{1,0:T(8,128)(2,1)} %fusion.q_ref.k_ref.v_ref, ...), custom_call_target="tpu_custom_call" | custom-call | tf_op jit(solution)/shard_map/attention_forward/pallas_call | solution.py:100
  108.3 3.4 slice.79.w_ref
  111.7 0.2 copy-done.12
  111.9 3.1 fusion.41
  115.0 0.5 multiply_reduce_fusion.2
  115.6 0.6 add_convert_fusion.x_ref
  116.2 0.6 copy-done.8
  116.8 15.9 %expand_forward.1 = (bf16[1190,3072]{1,0:T(8,128)(2,1)S(1)}, bf16[1190,3072]{1,0:T(8,128)(2,1)}) custom-call(bf16[1190,768]{1,0:T(8,128)(2,1)S(1)} %add_convert_fusion.x_ref, bf16[768,3072]{1,0:T(8,128)(2,1)S(1)} %slice.79.w_ref, f32[1,3072]{1,0:T(1,128)S(1)} %bitcast.26), custom_call_target="tpu_custom_call" | custom-call | tf_op jit(solution)/shard_map/expand_forward/pallas_call | solution.py:222
  132.7 3.1 copy-done.2
  135.8 9.3 %convolution_convert_fusion.2 = bf16[3072,768]{1,0:T(8,128)(2,1)} fusion(bf16[1190,3072]{1,0:T(8,128)(2,1)S(1)} %get-tuple-element.44, bf16[1190,768]{1,0:T(8,128)(2,1)S(1)} %copy-done.15, f32[1190]{0:T(1024)S(1)} %get-tuple-element.93), kind=kOutput, calls=%fused_computation.9 | convolution fusion | flops 5620225536 | bytes 13862552 | tf_op jit(solution)/shard_map/sf,sd->fd/dot_general | solution.py:556
  145.1 8.4 %all-gather.5.cloned.1.call-done = bf16[3072,768]{1,0:T(8,128)(2,1)} async-done(((bf16[96,768]{1,0:T(8,128)(2,1)}), bf16[3072,768]{1,0:T(8,128)(2,1)}) %all-gather.5.cloned.1.call-update) | async-done | bytes 4718608 | tf_op jit(solution)/shard_map/all_gather | solution.py:529
  153.6 12.2 %fusion.42 = (bf16[3072]{0:T(1024)(128)(2,1)}, bf16[1190,3072]{1,0:T(8,128)(2,1)}) fusion(bf16[1190,3072]{1,0:T(8,128)(2,1)} %get-tuple-element.46, bf16[3072,768]{1,0:T(8,128)(2,1)} %all-gather.5.cloned.1.call-done, bf16[1190,768]{1,0:T(8,128)(2,1)} %param.20, f32[1190]{0:T(1024)S(1)} %get-tuple-element.93), kind=kOutput, calls=%fused_computation.107 | convolution fusion | flops 5632485888 | bytes 21180056 | tf_op jit(solution)/shard_map/sd,fd->sf/dot_general | solution.py:561
  165.8 12.6 %multiply_reduce_fusion = (bf16[768]{0:T(1024)(128)(2,1)}, f32[1190]{0:T(1024)S(1)}, f32[1190]{0:T(1024)S(1)}, bf16[768]{0:T(1024)(128)(2,1)}, f32[1190,768]{1,0:T(8,128)S(1)}) fusion(f32[1190,768]{1,0:T(8,128)S(1)} %copy-done.9, f32[1190]{0:T(1024)S(1)} %add_rsqrt_fusion, f32[1190]{0:T(1024)S(1)} %broadcast_multiply_fusion.4, ...), kind=kOutput, calls=%fused_computation.27 | convolution fusion | flops 5623346176 | bytes 19378784 | tf_op jit(solution)/shard_map/sf,df->sd/dot_general | solution.py:569
  178.4 2.4 convert_reduce_fusion.1
  180.8 1.8 copy-done.14
  182.6 2.8 convolution_convert_fusion.4
  185.4 2.1 copy.50
  187.5 5.4 %convolution_convert_fusion.3.g_ref = bf16[1190,768]{1,0:T(8,128)(2,1)} fusion(bf16[768,3840]{1,0:T(8,128)(2,1)} %all-gather.3.cloned.1.call-done, f32[1190,768]{1,0:T(8,128)} %copy-done.14), kind=kOutput, calls=%fused_computation.37 | convolution fusion | flops 1405608960 | bytes 6669312 | tf_op jit(solution)/shard_map/se,de->sd/dot_general | solution.py:579
  192.8 75.7 %attention_backward.1 = (bf16[1190,768]{1,0:T(8,128)(2,1)}, bf16[1190,768]{1,0:T(8,128)(2,1)}, bf16[1190,768]{1,0:T(8,128)(2,1)}) custom-call(bf16[1190,2304]{1,0:T(8,128)(2,1)} %fusion.q_ref.k_ref.v_ref, bf16[1190,2304]{1,0:T(8,128)(2,1)} %fusion.q_ref.k_ref.v_ref, bf16[1190,2304]{1,0:T(8,128)(2,1)} %fusion.q_ref.k_ref.v_ref, ...), custom_call_target="tpu_custom_call" | custom-call | tf_op jit(solution)/shard_map/attention_backward/pallas_call | solution.py:186
  268.5 3.0 constant_dynamic-update-slice_fusion.2
  271.6 1.4 constant_dynamic-update-slice_fusion.1
  273.0 1.4 constant_dynamic-update-slice_fusion
  274.4 9.9 %convolution_convert_fusion.1 = bf16[768,3072]{1,0:T(8,128)(2,1)S(1)} fusion(bf16[1190,768]{1,0:T(8,128)(2,1)S(1)} %add_convert_fusion.x_ref, bf16[1190,3072]{1,0:T(8,128)(2,1)} %get-tuple-element.102), kind=kOutput, calls=%fused_computation.8 | convolution fusion | flops 5617483776 | bytes 13857792 | tf_op jit(solution)/shard_map/sd,sf->df/dot_general | solution.py:565
  284.4 2.9 pad_maximum_fusion
  287.3 2.0 copy-done.5
  289.3 10.8 %fusion.15 = (bf16[768]{0:T(1024)(128)(2,1)}, f32[1190]{0:T(1024)}, f32[1190]{0:T(1024)}, bf16[768]{0:T(1024)(128)(2,1)}, f32[1190,768]{1,0:T(8,128)}) fusion(bf16[1190,768]{1,0:T(8,128)(2,1)} %param.19, f32[1190]{0:T(1024)S(1)} %add_rsqrt_fusion.1, f32[1190]{0:T(1024)S(1)} %broadcast_multiply_fusion.5, f32[768]{0:T(1024)} %copy-done.28, ...), kind=kOutput, calls=%fused_computation.25 | convolution fusion | flops 4220478464 | bytes 14531168 | tf_op jit(solution)/shard_map/sc,dc->sd/dot_general | solution.py:590
  300.2 3.7 reduce
  304.1 0.2 copy.52
  304.3 0.7 pad.11.clone
  305.0 9.4 %convolution_convert_fusion = bf16[768,2304]{1,0:T(8,128)(2,1)} fusion(bf16[1190,2304]{1,0:T(8,128)(2,1)} %constant_dynamic-update-slice_fusion, bf16[1190,768]{1,0:T(8,128)(2,1)S(1)} %copy-done.13, f32[768]{0:T(1024)S(1)} %copy-done.40, f32[768]{0:T(1024)S(1)} %copy-done.29, f32[1190]{0:T(1024)S(1)} %add_rsqrt_fusion.1, f32[1190]{0:T(1024)S(1)} %broadcast_multiply_fusion.5), kind=kOutput, calls=%fused_computation.7 | convolution fusion | flops 4218596352 | bytes 10865968 | tf_op jit(solution)/shard_map/sd,sc->dc/dot_general | solution.py:586
  314.5 37.4 %scatter_sums.1 = (f32[24,2304]{1,0:T(8,128)}, f32[24,128]{1,0:T(8,128)}) custom-call(bf16[32,24,2304]{2,1,0:T(8,128)(2,1)} %bitcast.31, bf16[32,24,128]{2,1,0:T(8,128)(2,1)} %bitcast.32), custom_call_target="tpu_custom_call" | custom-call | tf_op jit(solution)/shard_map/scatter_sums/pallas_call | solution.py:456
  351.9 0.8 reshape.132
  352.8 0.6 fusion.34
  353.3 0.6 add_multiply_fusion.4
  353.9 1.8 fusion.38
  355.8 1.7 add_multiply_fusion.2
  357.5 5.8 %fusion.14 = f32[1190,768]{1,0:T(8,128)} fusion(f32[1190,768]{1,0:T(8,128)} %copy-done.14, bf16[1190,768]{1,0:T(8,128)(2,1)} %param.19, f32[1190,768]{1,0:T(8,128)} %get-tuple-element.100, f32[1190]{0:T(1024)S(1)} %broadcast_multiply_fusion, f32[1190]{0:T(1024)S(1)} %broadcast_multiply_fusion.1, f32[768]{0:T(1024)S(1)} %copy-done.29, ...), kind=kLoop, calls=%fused_computation.24 | loop fusion | flops 8225280 | bytes 12816992 | tf_op jit(solution)/shard_map/add | solution.py:594
  363.5 1.5 copy-done.10
  365.0 9.6 %fusion.19 = bf16[1190,768]{1,0:T(8,128)(2,1)} fusion(f32[1190,768]{1,0:T(8,128)S(1)} %copy-done.10, bf16[1190,3072]{1,0:T(8,128)(2,1)S(1)} %bitcast.28, bf16[3072,768]{1,0:T(8,128)(2,1)} %all-gather.5.cloned.1.call-done, f32[768]{0:T(1024)S(1)} %copy-done.38), kind=kOutput, calls=%fused_computation.36 | convolution fusion | flops 5617866240 | bytes 17516544 | tf_op jit(solution)/shard_map/dot_general | solution.py:550
  374.6 2.0 fusion.35
  376.6 1.8 add_multiply_fusion
  378.4 26.2 %reduce-scatter.3.cloned.1.call-done = bf16[24,3840]{1,0:T(8,128)(2,1)} async-done(((bf16[768,3840]{1,0:T(8,128)(2,1)}), bf16[24,3840]{1,0:T(8,128)(2,1)}) %reduce-scatter.3.cloned.1.call-update) | async-done | bytes 184336 | tf_op jit(solution)/shard_map/reduce_scatter | solution.py:611
  404.6 1.6 fusion.37
  406.1 1.6 add_multiply_fusion.3
  407.7 2.0 fusion.36
  409.7 0.8 add_multiply_fusion.1
  410.5 0.7 copy.57
  (130 shorter events, 0.8 us)
Async XLA Ops:
  7.2 48.0 %copy-start.11 = (bf16[1190,768]{1,0:T(8,128)(2,1)S(1)}, bf16[1190,768]{1,0:T(8,128)(2,1)}, u32[]{:S(2)}) copy-start(bf16[1190,768]{1,0:T(8,128)(2,1)} %param.19) | copy-start | bytes 5483524
  7.2 101.1 %all-gather.3.cloned.1.call-start = ((), (), s32[]{:S(2)}) async-start(), calls=%async_computation.2 | async-start | bytes 6082560 | tf_op jit(solution)/shard_map/all_gather | solution.py:528
  10.0 143.5 %all-gather.5.cloned.1.call-start = ((), (), s32[]{:S(2)}) async-start(), calls=%async_computation.3 | async-start | bytes 4866048 | tf_op jit(solution)/shard_map/all_gather | solution.py:529
  11.7 362.9 %reduce-scatter.5.cloned.1.call-start = ((), (), s32[]{:S(2)}) async-start(), calls=%async_computation.5 | async-start | bytes 4866048 | tf_op jit(solution)/shard_map/reduce_scatter | solution.py:610
  49.0 1.8 copy-start.3
  50.9 5.7 %copy-start.4 = (bf16[32,24,2304]{2,1,0:T(8,128)(2,1)S(1)}, bf16[32,24,2304]{2,1,0:T(8,128)(2,1)}, u32[]{:S(2)}) copy-start(bf16[32,24,2304]{2,1,0:T(8,128)(2,1)} %copy-done.3) | copy-start | bytes 10616836
  55.2 8.1 %copy-start.28 = (f32[768]{0:T(1024)}, f32[768]{0:T(1024)S(1)}, u32[]{:S(2)}) copy-start(f32[768]{0:T(1024)S(1)} %get-tuple-element.70) | copy-start | bytes 9220
  55.2 8.1 %copy-start.39 = (f32[768]{0:T(1024)}, f32[768]{0:T(1024)S(1)}, u32[]{:S(2)}) copy-start(f32[768]{0:T(1024)S(1)} %get-tuple-element.69) | copy-start | bytes 9220
  56.6 6.8 %copy-start = (bf16[1280,128]{1,0:T(8,128)(2,1)}, bf16[1280,128]{1,0:T(8,128)(2,1)S(1)}, u32[]{:S(2)}) copy-start(bf16[1280,128]{1,0:T(8,128)(2,1)S(1)} %get-tuple-element.91.fk_ref) | copy-start | bytes 983044
  56.6 6.8 %copy-start.1 = (bf16[1280,128]{1,0:T(8,128)(2,1)}, bf16[1280,128]{1,0:T(8,128)(2,1)S(1)}, u32[]{:S(2)}) copy-start(bf16[1280,128]{1,0:T(8,128)(2,1)S(1)} %get-tuple-element.92.fq_ref) | copy-start | bytes 983044
  108.3 3.4 copy-start.6
  108.3 3.6 copy-start.12
  115.0 1.8 copy-start.8
  116.8 19.0 %copy-start.15 = (bf16[1190,768]{1,0:T(8,128)(2,1)S(1)}, bf16[1190,768]{1,0:T(8,128)(2,1)}, u32[]{:S(2)}) copy-start(bf16[1190,768]{1,0:T(8,128)(2,1)} %param.20) | copy-start | bytes 5483524
  132.7 3.1 copy-start.2
  153.5 251.0 %reduce-scatter.3.cloned.1.call-start = ((), (), s32[]{:S(2)}) async-start(), calls=%async_computation.4 | async-start | bytes 6082560 | tf_op jit(solution)/shard_map/reduce_scatter | solution.py:611
  153.6 12.3 %copy-start.9 = (f32[1190,768]{1,0:T(8,128)S(1)}, f32[1190,768]{1,0:T(8,128)}, u32[]{:S(2)}) copy-start(f32[1190,768]{1,0:T(8,128)} %copy-done.8) | copy-start | bytes 10967044
  165.8 12.6 %copy-start.16 = (bf16[1190,768]{1,0:T(8,128)(2,1)S(1)}, bf16[1190,768]{1,0:T(8,128)(2,1)}, u32[]{:S(2)}) copy-start(bf16[1190,768]{1,0:T(8,128)(2,1)} %param.20) | copy-start | bytes 5483524
  178.4 4.2 %copy-start.7 = (bf16[1190,768]{1,0:T(8,128)(2,1)S(1)}, bf16[1190,768]{1,0:T(8,128)(2,1)}, u32[]{:S(2)}) copy-start(bf16[1190,768]{1,0:T(8,128)(2,1)} %copy-done.6) | copy-start | bytes 5483524
  180.8 1.8 copy-start.14
  268.5 3.1 copy-start.18
  268.5 4.5 %copy-start.17 = (bf16[1190,768]{1,0:T(8,128)(2,1)S(1)}, bf16[1190,768]{1,0:T(8,128)(2,1)}, u32[]{:S(2)}) copy-start(bf16[1190,768]{1,0:T(8,128)(2,1)} %get-tuple-element.51) | copy-start | bytes 5483524
  287.3 2.0 copy-start.5
  300.1 3.8 copy-start.45
  300.1 3.8 copy-start.44
  300.1 3.8 copy-start.36
  300.1 3.9 copy-start.43
  300.1 3.9 copy-start.42
  300.1 3.9 copy-start.37
  300.1 3.9 copy-start.30
  300.1 4.9 %copy-start.13 = (bf16[1190,768]{1,0:T(8,128)(2,1)S(1)}, bf16[1190,768]{1,0:T(8,128)(2,1)}, u32[]{:S(2)}) copy-start(bf16[1190,768]{1,0:T(8,128)(2,1)} %param.19) | copy-start | bytes 5483524
  300.1 4.9 %copy-start.29 = (f32[768]{0:T(1024)S(1)}, f32[768]{0:T(1024)}, u32[]{:S(2)}) copy-start(f32[768]{0:T(1024)} %copy-done.28) | copy-start | bytes 9220
  300.2 4.9 %copy-start.40 = (f32[768]{0:T(1024)S(1)}, f32[768]{0:T(1024)}, u32[]{:S(2)}) copy-start(f32[768]{0:T(1024)} %copy-done.39) | copy-start | bytes 9220
  314.4 38.3 %copy-start.35 = (f32[288]{0:T(512)S(1)}, f32[288]{0:T(512)}, u32[]{:S(2)}) copy-start(f32[288]{0:T(512)} %param.35) | copy-start | bytes 3460
  314.4 38.3 %copy-start.46 = (f32[288]{0:T(512)S(1)}, f32[288]{0:T(512)}, u32[]{:S(2)}) copy-start(f32[288]{0:T(512)} %param.36) | copy-start | bytes 3460
  314.4 38.9 %copy-start.41 = (f32[288]{0:T(512)S(1)}, f32[288]{0:T(512)}, u32[]{:S(2)}) copy-start(f32[288]{0:T(512)} %param.37) | copy-start | bytes 3460
  314.4 39.5 %copy-start.32 = (f32[1190]{0:T(1024)S(1)}, f32[1190]{0:T(1024)}, u32[]{:S(2)}) copy-start(f32[1190]{0:T(1024)} %get-tuple-element.58) | copy-start | bytes 14284
  314.4 39.5 %copy-start.31 = (f32[1190]{0:T(1024)S(1)}, f32[1190]{0:T(1024)}, u32[]{:S(2)}) copy-start(f32[1190]{0:T(1024)} %get-tuple-element.59) | copy-start | bytes 14284
  314.5 39.5 %copy-start.23 = (f32[24,2304]{1,0:T(8,128)S(1)}, f32[24,2304]{1,0:T(8,128)}, u32[]{:S(2)}) copy-start(f32[24,2304]{1,0:T(8,128)} %param.23) | copy-start | bytes 663556
  314.5 48.9 %slice-start = ((s8[7323648]{0:T(1024)(128)(4,1)}), s8[3129344]{0:T(1024)(128)(4,1)S(1)}, s32[]{:S(2)}) async-start(s8[7323648]{0:T(1024)(128)(4,1)} %bitcast.27), calls=%async_computation.6 | async-start | bytes 6258688
  352.7 10.6 %copy-start.33 = (f32[288]{0:T(512)}, f32[288]{0:T(512)S(1)}, u32[]{:S(2)}) copy-start(f32[288]{0:T(512)S(1)} %reshape.132) | copy-start | bytes 3460
  353.3 10.0 %copy-start.34 = (f32[288]{0:T(512)}, f32[288]{0:T(512)S(1)}, u32[]{:S(2)}) copy-start(f32[288]{0:T(512)S(1)} %get-tuple-element.156) | copy-start | bytes 3460
  355.8 1.7 copy-start.24
  357.5 5.9 %slice-start.1 = ((s8[7323648]{0:T(1024)(128)(4,1)}), s8[4194304]{0:T(1024)(128)(4,1)S(1)}, s32[]{:S(2)}) async-start(s8[7323648]{0:T(1024)(128)(4,1)} %bitcast.27), calls=%async_computation.7 | async-start | bytes 8388608
  357.5 7.4 %copy-start.10 = (f32[1190,768]{1,0:T(8,128)S(1)}, f32[1190,768]{1,0:T(8,128)}, u32[]{:S(2)}) copy-start(f32[1190,768]{1,0:T(8,128)} %copy-done.8) | copy-start | bytes 10967044
  357.5 7.4 %copy-start.38 = (f32[768]{0:T(1024)S(1)}, f32[768]{0:T(1024)}, u32[]{:S(2)}) copy-start(f32[768]{0:T(1024)} %get-tuple-element.63) | copy-start | bytes 9220
  365.0 9.6 %copy-start.20 = (f32[96,768]{1,0:T(8,128)S(1)}, f32[96,768]{1,0:T(8,128)}, u32[]{:S(2)}) copy-start(f32[96,768]{1,0:T(8,128)} %param.32) | copy-start | bytes 884740
  365.0 39.6 %copy-start.27 = (f32[24,768]{1,0:T(8,128)S(1)}, f32[24,768]{1,0:T(8,128)}, u32[]{:S(2)}) copy-start(f32[24,768]{1,0:T(8,128)} %param.26) | copy-start | bytes 221188
  374.6 35.1 %copy-start.25 = (f32[24,3072]{1,0:T(8,128)S(1)}, f32[24,3072]{1,0:T(8,128)}, u32[]{:S(2)}) copy-start(f32[24,3072]{1,0:T(8,128)} %param.31) | copy-start | bytes 884740
  374.6 35.9 %copy-start.22 = (f32[24,2304]{1,0:T(8,128)S(1)}, f32[24,2304]{1,0:T(8,128)}, u32[]{:S(2)}) copy-start(f32[24,2304]{1,0:T(8,128)} %get-tuple-element.134) | copy-start | bytes 663556
  376.6 34.6 %copy-start.19 = (f32[96,768]{1,0:T(8,128)}, f32[96,768]{1,0:T(8,128)S(1)}, u32[]{:S(2)}) copy-start(f32[96,768]{1,0:T(8,128)S(1)} %get-tuple-element.151) | copy-start | bytes 884740
  406.1 5.1 %copy-start.26 = (f32[24,768]{1,0:T(8,128)}, f32[24,768]{1,0:T(8,128)S(1)}, u32[]{:S(2)}) copy-start(f32[24,768]{1,0:T(8,128)S(1)} %get-tuple-element.141) | copy-start | bytes 221188
  409.7 1.5 copy-start.21
Sparse Core Ops, SparseCore 0:
  11.5 76.3 all-gather.2
  91.3 62.1 all-gather.4
  159.0 106.2 reduce-scatter.4
  287.4 117.0 reduce-scatter.2
